TPU v7x, 32 devices: a whole 2x2x4 slice. The times are simulated.
32 devices in a mesh: dp: 8 (over z, x), fsdp: 4 (over y, core).
Axes of the slice: x: 2, y: 2, z: 4, core: 2. Of those that a mesh axis runs over, the one named last changes fastest.
Arguments:
- tokens: bfloat16 [32768, 768], P(('dp', 'fsdp')), may hold values from -6 to 6
- seg_lengths: int32 [32, 8], P(('dp', 'fsdp')), may hold values from 1 to 768, 1024 in all within a row
- cotangent: bfloat16 [32768, 768], P(('dp', 'fsdp')), may hold values from -6 to 6
- in_gain: bfloat16 [768], P(('dp', 'fsdp')), may hold values from 0.5 to 1.5
- in_bias: bfloat16 [768], P(('dp', 'fsdp')), may hold values from -1 to 1
- qkv_weight: bfloat16 [768, 2304], P(('dp', 'fsdp')), may hold values from -0.21875 to 0.21875
- qv_bias: bfloat16 [1536], P(('dp', 'fsdp')), may hold values from -1 to 1
- mid_gain: bfloat16 [768], P(('dp', 'fsdp')), may hold values from 0.5 to 1.5
- mid_bias: bfloat16 [768], P(('dp', 'fsdp')), may hold values from -1 to 1
- out_weight: bfloat16 [768, 768], P(('dp', 'fsdp')), may hold values from -0.21875 to 0.21875
- out_bias: bfloat16 [768], P(('dp', 'fsdp')), may hold values from -1 to 1
- ffn_gain: bfloat16 [768], P(('dp', 'fsdp')), may hold values from 0.5 to 1.5
- ffn_bias: bfloat16 [768], P(('dp', 'fsdp')), may hold values from -1 to 1
- up_weight: bfloat16 [768, 3072], P(('dp', 'fsdp')), may hold values from -0.21875 to 0.21875
- up_bias: bfloat16 [3072], P(('dp', 'fsdp')), may hold values from -1 to 1
- hid_gain: bfloat16 [3072], P(('dp', 'fsdp')), may hold values from 0.5 to 1.5
- hid_bias: bfloat16 [3072], P(('dp', 'fsdp')), may hold values from -1 to 1
- down_weight: bfloat16 [3072, 768], P(('dp', 'fsdp')), may hold values from -0.109375 to 0.109375
- down_bias: bfloat16 [768], P(('dp', 'fsdp')), may hold values from -1 to 1
Outputs:
- out_tokens: bfloat16 [32768, 768], P(('dp', 'fsdp'))
- grad_tokens: float32 [32768, 768], P(('dp', 'fsdp'))
- grad_in_gain: float32 [768], P(('dp', 'fsdp'))
- grad_in_bias: float32 [768], P(('dp', 'fsdp'))
- grad_qkv_weight: float32 [768, 2304], P(('dp', 'fsdp'))
- grad_qv_bias: float32 [1536], P(('dp', 'fsdp'))
- grad_mid_gain: float32 [768], P(('dp', 'fsdp'))
- grad_mid_bias: float32 [768], P(('dp', 'fsdp'))
- grad_out_weight: float32 [768, 768], P(('dp', 'fsdp'))
- grad_out_bias: float32 [768], P(('dp', 'fsdp'))
- grad_ffn_gain: float32 [768], P(('dp', 'fsdp'))
- grad_ffn_bias: float32 [768], P(('dp', 'fsdp'))
- grad_up_weight: float32 [768, 3072], P(('dp', 'fsdp'))
- grad_up_bias: float32 [3072], P(('dp', 'fsdp'))
- grad_hid_gain: float32 [3072], P(('dp', 'fsdp'))
- grad_hid_bias: float32 [3072], P(('dp', 'fsdp'))
- grad_down_weight: float32 [3072, 768], P(('dp', 'fsdp'))
- grad_down_bias: float32 [768], P(('dp', 'fsdp'))
Inputs may be any that keep to these rules, and one draw needn't show every extreme that they name: `seg_lengths`: each row's 8 entries are the lengths of its packed sequences in slot order, the last entry being the padding run at the row's end; they sum to 1024, and some entry equals 768.
All inputs are finite; a program needn't handle non-finite values.
Results may differ from a plain program's by a relative error of at most 0.012.
Values may be sent and summed in bfloat16 or wider, within the bound.
No kernel may reach another device: no remote copies, remote signals or barrier semaphores. Data moves between devices by JAX's collectives and lax.ppermute only.
A program may use at most 256 MiB of HBM per device.

v0:
```python
import math

import jax
import jax.numpy as jnp
from jax import lax
from jax.sharding import PartitionSpec as P

HD = 64
ROW = 1024
BLOCK = 512


EPSILON = 1e-05
NEGATIVE = -1e30


def layer_norm(inputs, norm_gain, norm_bias):
    center = inputs - jnp.mean(inputs, axis=-1, keepdims=True)
    spread = jnp.mean(center * center, axis=-1, keepdims=True)
    return center * lax.rsqrt(spread + EPSILON) * norm_gain + norm_bias


def gelu_norm(inputs, norm_gain, norm_bias):
    return layer_norm(jax.nn.gelu(inputs, approximate=False), norm_gain, norm_bias)


def product(left, right):
    return jnp.dot(left, right, preferred_element_type=jnp.float32)


def product_tn(left, right):
    return lax.dot_general(
        left, right, (((0,), (0,)), ((), ())), preferred_element_type=jnp.float32
    )


def product_nt(left, right):
    return lax.dot_general(
        left, right, (((1,), (1,)), ((), ())), preferred_element_type=jnp.float32
    )


def segment_ids(lengths, slots):
    segment_ends = jnp.cumsum(lengths)[:-1]
    token_positions = jnp.arange(slots, dtype=jnp.int32)
    return jnp.sum((token_positions[:, None] >= segment_ends[None, :]).astype(jnp.int32), axis=1)


def visible_pair_grid(document_ids, query_position_index, key_position_index, window_extent):
    token_positions = jnp.arange(window_extent, dtype=jnp.int32)
    query_segment = document_ids[
        query_position_index * window_extent : (query_position_index + 1) * window_extent
    ]
    key_document_ids = document_ids[
        key_position_index * window_extent : (key_position_index + 1) * window_extent
    ]
    same = query_segment[:, None] == key_document_ids[None, :]
    causal_ordering = (
        key_position_index * window_extent + token_positions[None, :]
        <= query_position_index * window_extent + token_positions[:, None]
    )
    return (same & causal_ordering)[None]


def block_scores(query_block, key_tile_rows, factor):
    return (
        jnp.einsum("qhd,khd->hqk", query_block, key_tile_rows, preferred_element_type=jnp.float32)
        * factor
    )


def attend_forward(query_rows, key_row_slice, value_row_slice, document_ids, window_extent):
    factor = 1.0 / math.sqrt(query_rows.shape[2])
    block_count = query_rows.shape[0] // window_extent
    head_count = query_rows.shape[1]
    outputs = []
    totals = []
    for query_position_index in range(block_count):
        query_block = query_rows[
            query_position_index * window_extent : (query_position_index + 1) * window_extent
        ]
        top = jnp.full((head_count, window_extent), NEGATIVE, jnp.float32)
        mass = jnp.zeros((head_count, window_extent), jnp.float32)
        for key_position_index in range(query_position_index + 1):
            key_tile_rows = key_row_slice[
                key_position_index * window_extent : (key_position_index + 1) * window_extent
            ]
            scores = block_scores(query_block, key_tile_rows, factor)
            permitted_pairs_mask = visible_pair_grid(
                document_ids, query_position_index, key_position_index, window_extent
            )
            masked = jnp.where(permitted_pairs_mask, scores, NEGATIVE)
            newest = jnp.maximum(top, jnp.max(masked, axis=-1))
            fresh = jnp.where(permitted_pairs_mask, jnp.exp(masked - newest[:, :, None]), 0.0)
            mass = mass * jnp.exp(top - newest) + jnp.sum(fresh, axis=-1)
            top = newest
        log_total = top + jnp.log(mass)
        accum = jnp.zeros((window_extent, head_count, query_rows.shape[2]), jnp.float32)
        for key_position_index in range(query_position_index + 1):
            key_tile_rows = key_row_slice[
                key_position_index * window_extent : (key_position_index + 1) * window_extent
            ]
            value_tile_rows = value_row_slice[
                key_position_index * window_extent : (key_position_index + 1) * window_extent
            ]
            scores = block_scores(query_block, key_tile_rows, factor)
            permitted_pairs_mask = visible_pair_grid(
                document_ids, query_position_index, key_position_index, window_extent
            )
            soft_low = jnp.where(
                permitted_pairs_mask, jnp.exp(scores - log_total[:, :, None]), 0.0
            ).astype(jnp.bfloat16)
            accum = accum + jnp.einsum(
                "hqk,khd->qhd", soft_low, value_tile_rows, preferred_element_type=jnp.float32
            )
        outputs.append(accum)
        totals.append(log_total)
    return (jnp.concatenate(outputs, axis=0), totals)


def attend_backward(
    query_rows,
    key_row_slice,
    value_row_slice,
    document_ids,
    totals,
    grad_out,
    attended,
    window_extent,
):
    factor = 1.0 / math.sqrt(query_rows.shape[2])
    block_count = query_rows.shape[0] // window_extent
    row_delta = jnp.einsum("qhd,qhd->hq", grad_out.astype(jnp.float32), attended)
    zero_block = jnp.zeros((window_extent,) + query_rows.shape[1:], jnp.float32)
    grad_query = [zero_block for index in range(block_count)]
    key_gradient = [zero_block for index in range(block_count)]
    value_gradient = [zero_block for index in range(block_count)]
    for query_position_index in range(block_count):
        query_block = query_rows[
            query_position_index * window_extent : (query_position_index + 1) * window_extent
        ]
        grad_block = grad_out[
            query_position_index * window_extent : (query_position_index + 1) * window_extent
        ]
        delta_block = row_delta[
            :, query_position_index * window_extent : (query_position_index + 1) * window_extent
        ]
        for key_position_index in range(query_position_index + 1):
            key_tile_rows = key_row_slice[
                key_position_index * window_extent : (key_position_index + 1) * window_extent
            ]
            value_tile_rows = value_row_slice[
                key_position_index * window_extent : (key_position_index + 1) * window_extent
            ]
            scores = block_scores(query_block, key_tile_rows, factor)
            permitted_pairs_mask = visible_pair_grid(
                document_ids, query_position_index, key_position_index, window_extent
            )
            soft = jnp.where(
                permitted_pairs_mask,
                jnp.exp(scores - totals[query_position_index][:, :, None]),
                0.0,
            )
            value_gradient[key_position_index] = value_gradient[key_position_index] + jnp.einsum(
                "hqk,qhd->khd",
                soft.astype(jnp.bfloat16),
                grad_block,
                preferred_element_type=jnp.float32,
            )
            grad_soft = jnp.einsum(
                "qhd,khd->hqk", grad_block, value_tile_rows, preferred_element_type=jnp.float32
            )
            grad_scores = (soft * (grad_soft - delta_block[:, :, None])).astype(jnp.bfloat16)
            grad_query[query_position_index] = (
                grad_query[query_position_index]
                + jnp.einsum(
                    "hqk,khd->qhd", grad_scores, key_tile_rows, preferred_element_type=jnp.float32
                )
                * factor
            )
            key_gradient[key_position_index] = (
                key_gradient[key_position_index]
                + jnp.einsum(
                    "hqk,qhd->khd", grad_scores, query_block, preferred_element_type=jnp.float32
                )
                * factor
            )
    return (
        jnp.concatenate(grad_query, axis=0),
        jnp.concatenate(key_gradient, axis=0),
        jnp.concatenate(value_gradient, axis=0),
    )


def body(
    tokens,
    seg_lengths,
    cotangent,
    in_gain,
    in_bias,
    qkv_weight,
    qv_bias,
    mid_gain,
    mid_bias,
    out_weight,
    out_bias,
    ffn_gain,
    ffn_bias,
    up_weight,
    up_bias,
    hid_gain,
    hid_bias,
    down_weight,
    down_bias,
):
    gathered = (
        lax.all_gather(in_gain, ("dp", "fsdp"), axis=0, tiled=True),
        lax.all_gather(in_bias, ("dp", "fsdp"), axis=0, tiled=True),
        lax.all_gather(qkv_weight, ("dp", "fsdp"), axis=0, tiled=True),
        lax.all_gather(qv_bias, ("dp", "fsdp"), axis=0, tiled=True),
        lax.all_gather(mid_gain, ("dp", "fsdp"), axis=0, tiled=True),
        lax.all_gather(mid_bias, ("dp", "fsdp"), axis=0, tiled=True),
        lax.all_gather(out_weight, ("dp", "fsdp"), axis=0, tiled=True),
        lax.all_gather(out_bias, ("dp", "fsdp"), axis=0, tiled=True),
        lax.all_gather(ffn_gain, ("dp", "fsdp"), axis=0, tiled=True),
        lax.all_gather(ffn_bias, ("dp", "fsdp"), axis=0, tiled=True),
        lax.all_gather(up_weight, ("dp", "fsdp"), axis=0, tiled=True),
        lax.all_gather(up_bias, ("dp", "fsdp"), axis=0, tiled=True),
        lax.all_gather(hid_gain, ("dp", "fsdp"), axis=0, tiled=True),
        lax.all_gather(hid_bias, ("dp", "fsdp"), axis=0, tiled=True),
        lax.all_gather(down_weight, ("dp", "fsdp"), axis=0, tiled=True),
        lax.all_gather(down_bias, ("dp", "fsdp"), axis=0, tiled=True),
    )
    model_width = tokens.shape[1]
    head_count = model_width // HD
    block_count = ROW // BLOCK
    in_gain_full = gathered[0].astype(jnp.float32)
    in_bias_full = gathered[1].astype(jnp.float32)
    qv_full = gathered[3].astype(jnp.float32)
    mid_gain_full = gathered[4].astype(jnp.float32)
    mid_bias_full = gathered[5].astype(jnp.float32)
    out_bias_full = gathered[7].astype(jnp.float32)
    ffn_gain_full = gathered[8].astype(jnp.float32)
    ffn_bias_full = gathered[9].astype(jnp.float32)
    up_bias_full = gathered[11].astype(jnp.float32)
    hid_gain_full = gathered[12].astype(jnp.float32)
    hid_bias_full = gathered[13].astype(jnp.float32)
    down_bias_full = gathered[15].astype(jnp.float32)
    qkv_bias_full = jnp.concatenate(
        [qv_full[:model_width], jnp.zeros((model_width,), jnp.float32), qv_full[model_width:]]
    )
    row_index = 0
    row_inputs = tokens.astype(jnp.float32)
    document_ids = segment_ids(seg_lengths[row_index], ROW)
    normed_one, in_back = jax.vjp(layer_norm, row_inputs, in_gain_full, in_bias_full)
    hidden_one = normed_one.astype(jnp.bfloat16)
    projected = (product(hidden_one, gathered[2]) + qkv_bias_full).astype(jnp.bfloat16)
    query_rows = projected[:, :model_width].reshape(ROW, head_count, HD)
    key_row_slice = projected[:, model_width : 2 * model_width].reshape(ROW, head_count, HD)
    value_row_slice = projected[:, 2 * model_width :].reshape(ROW, head_count, HD)
    attended, totals = attend_forward(
        query_rows, key_row_slice, value_row_slice, document_ids, BLOCK
    )
    normed_two, mid_back = jax.vjp(
        layer_norm, attended.reshape(ROW, model_width), mid_gain_full, mid_bias_full
    )
    hidden_two = normed_two.astype(jnp.bfloat16)
    middle = row_inputs + product(hidden_two, gathered[6]) + out_bias_full
    ffn_kept = []
    out_blocks = []
    for bindex in range(block_count):
        middle_block = middle[bindex * BLOCK : (bindex + 1) * BLOCK]
        normed_three, ffn_back = jax.vjp(layer_norm, middle_block, ffn_gain_full, ffn_bias_full)
        hidden_three = normed_three.astype(jnp.bfloat16)
        upward = product(hidden_three, gathered[10]) + up_bias_full
        normed_four, hid_back = jax.vjp(gelu_norm, upward, hid_gain_full, hid_bias_full)
        hidden_four = normed_four.astype(jnp.bfloat16)
        out_blocks.append(middle_block + product(hidden_four, gathered[14]) + down_bias_full)
        ffn_kept.append((ffn_back, hidden_three, hid_back, hidden_four))
    out_rows = jnp.concatenate(out_blocks, axis=0).astype(jnp.bfloat16)
    kept_rows = [
        (
            in_back,
            hidden_one,
            query_rows,
            key_row_slice,
            value_row_slice,
            document_ids,
            totals,
            attended,
            mid_back,
            hidden_two,
            ffn_kept,
        )
    ]
    weights_back = (
        lax.all_gather(in_gain, ("dp", "fsdp"), axis=0, tiled=True),
        lax.all_gather(in_bias, ("dp", "fsdp"), axis=0, tiled=True),
        lax.all_gather(qkv_weight, ("dp", "fsdp"), axis=0, tiled=True),
        lax.all_gather(qv_bias, ("dp", "fsdp"), axis=0, tiled=True),
        lax.all_gather(mid_gain, ("dp", "fsdp"), axis=0, tiled=True),
        lax.all_gather(mid_bias, ("dp", "fsdp"), axis=0, tiled=True),
        lax.all_gather(out_weight, ("dp", "fsdp"), axis=0, tiled=True),
        lax.all_gather(out_bias, ("dp", "fsdp"), axis=0, tiled=True),
        lax.all_gather(ffn_gain, ("dp", "fsdp"), axis=0, tiled=True),
        lax.all_gather(ffn_bias, ("dp", "fsdp"), axis=0, tiled=True),
        lax.all_gather(up_weight, ("dp", "fsdp"), axis=0, tiled=True),
        lax.all_gather(up_bias, ("dp", "fsdp"), axis=0, tiled=True),
        lax.all_gather(hid_gain, ("dp", "fsdp"), axis=0, tiled=True),
        lax.all_gather(hid_bias, ("dp", "fsdp"), axis=0, tiled=True),
        lax.all_gather(down_weight, ("dp", "fsdp"), axis=0, tiled=True),
        lax.all_gather(down_bias, ("dp", "fsdp"), axis=0, tiled=True),
    )
    acc_ffn_gain = jnp.zeros(ffn_gain_full.shape, jnp.float32)
    acc_ffn_bias = jnp.zeros(ffn_gain_full.shape, jnp.float32)
    acc_up_weight = jnp.zeros(gathered[10].shape, jnp.float32)
    acc_up_bias = jnp.zeros(up_bias_full.shape, jnp.float32)
    acc_hid_gain = jnp.zeros(hid_gain_full.shape, jnp.float32)
    acc_hid_bias = jnp.zeros(hid_gain_full.shape, jnp.float32)
    acc_down_weight = jnp.zeros(gathered[14].shape, jnp.float32)
    acc_down_bias = jnp.zeros(down_bias_full.shape, jnp.float32)
    row_index = 0
    ffn_kept = kept_rows[row_index][10]
    grad_blocks = []
    for bindex in range(block_count):
        ffn_back, hidden_three, hid_back, hidden_four = ffn_kept[bindex]
        start = row_index * ROW + bindex * BLOCK
        grad_final = cotangent[start : start + BLOCK].astype(jnp.float32)
        grad_low = grad_final.astype(jnp.bfloat16)
        acc_down_bias = acc_down_bias + jnp.sum(grad_low.astype(jnp.float32), axis=0)
        acc_down_weight = acc_down_weight + product_tn(hidden_four, grad_low)
        grad_four = product_nt(grad_low, weights_back[14])
        grad_up, part_gain, part_bias = hid_back(grad_four)
        acc_hid_gain = acc_hid_gain + part_gain
        acc_hid_bias = acc_hid_bias + part_bias
        grad_up_low = grad_up.astype(jnp.bfloat16)
        acc_up_bias = acc_up_bias + jnp.sum(grad_up_low.astype(jnp.float32), axis=0)
        acc_up_weight = acc_up_weight + product_tn(hidden_three, grad_up_low)
        grad_three = product_nt(grad_up_low, weights_back[10])
        grad_mid_part, part_gain, part_bias = ffn_back(grad_three)
        acc_ffn_gain = acc_ffn_gain + part_gain
        acc_ffn_bias = acc_ffn_bias + part_bias
        grad_blocks.append(grad_final + grad_mid_part)
    grad_middle_rows = [jnp.concatenate(grad_blocks, axis=0)]
    row_index = 0
    (
        in_back,
        hidden_one,
        query_rows,
        key_row_slice,
        value_row_slice,
        document_ids,
        totals,
        attended,
        mid_back,
        hidden_two,
        ffn_kept,
    ) = kept_rows[row_index]
    grad_middle = grad_middle_rows[row_index]
    grad_branch = grad_middle.astype(jnp.bfloat16)
    acc_out_bias = jnp.sum(grad_branch.astype(jnp.float32), axis=0)
    acc_out_weight = product_tn(hidden_two, grad_branch)
    grad_two = product_nt(grad_branch, weights_back[6])
    grad_attended, part_gain, part_bias = mid_back(grad_two)
    acc_mid_gain = part_gain
    acc_mid_bias = part_bias
    grad_att_low = grad_attended.astype(jnp.bfloat16).reshape(ROW, head_count, HD)
    grad_query, key_gradient, value_gradient = attend_backward(
        query_rows,
        key_row_slice,
        value_row_slice,
        document_ids,
        totals,
        grad_att_low,
        attended,
        BLOCK,
    )
    grad_projected = jnp.concatenate(
        [
            grad_query.reshape(ROW, model_width),
            key_gradient.reshape(ROW, model_width),
            value_gradient.reshape(ROW, model_width),
        ],
        axis=1,
    ).astype(jnp.bfloat16)
    column_sums = jnp.sum(grad_projected.astype(jnp.float32), axis=0)
    acc_qv_bias = jnp.concatenate([column_sums[:model_width], column_sums[2 * model_width :]])
    acc_qkv_weight = product_tn(hidden_one, grad_projected)
    grad_one = product_nt(grad_projected, weights_back[2])
    grad_input_part, part_gain, part_bias = in_back(grad_one)
    grad_rows = grad_middle + grad_input_part
    summed = (
        lax.psum_scatter(part_gain, ("dp", "fsdp"), scatter_dimension=0, tiled=True),
        lax.psum_scatter(part_bias, ("dp", "fsdp"), scatter_dimension=0, tiled=True),
        lax.psum_scatter(acc_qkv_weight, ("dp", "fsdp"), scatter_dimension=0, tiled=True),
        lax.psum_scatter(acc_qv_bias, ("dp", "fsdp"), scatter_dimension=0, tiled=True),
        lax.psum_scatter(acc_mid_gain, ("dp", "fsdp"), scatter_dimension=0, tiled=True),
        lax.psum_scatter(acc_mid_bias, ("dp", "fsdp"), scatter_dimension=0, tiled=True),
        lax.psum_scatter(acc_out_weight, ("dp", "fsdp"), scatter_dimension=0, tiled=True),
        lax.psum_scatter(acc_out_bias, ("dp", "fsdp"), scatter_dimension=0, tiled=True),
        lax.psum_scatter(acc_ffn_gain, ("dp", "fsdp"), scatter_dimension=0, tiled=True),
        lax.psum_scatter(acc_ffn_bias, ("dp", "fsdp"), scatter_dimension=0, tiled=True),
        lax.psum_scatter(acc_up_weight, ("dp", "fsdp"), scatter_dimension=0, tiled=True),
        lax.psum_scatter(acc_up_bias, ("dp", "fsdp"), scatter_dimension=0, tiled=True),
        lax.psum_scatter(acc_hid_gain, ("dp", "fsdp"), scatter_dimension=0, tiled=True),
        lax.psum_scatter(acc_hid_bias, ("dp", "fsdp"), scatter_dimension=0, tiled=True),
        lax.psum_scatter(acc_down_weight, ("dp", "fsdp"), scatter_dimension=0, tiled=True),
        lax.psum_scatter(acc_down_bias, ("dp", "fsdp"), scatter_dimension=0, tiled=True),
    )
    return (
        out_rows,
        grad_rows,
        summed[0],
        summed[1],
        summed[2],
        summed[3],
        summed[4],
        summed[5],
        summed[6],
        summed[7],
        summed[8],
        summed[9],
        summed[10],
        summed[11],
        summed[12],
        summed[13],
        summed[14],
        summed[15],
    )


def solution(mesh):
    in_specs = (
        P(("dp", "fsdp"), None),
        P(("dp", "fsdp"), None),
        P(("dp", "fsdp"), None),
        P(("dp", "fsdp")),
        P(("dp", "fsdp")),
        P(("dp", "fsdp"), None),
        P(("dp", "fsdp")),
        P(("dp", "fsdp")),
        P(("dp", "fsdp")),
        P(("dp", "fsdp"), None),
        P(("dp", "fsdp")),
        P(("dp", "fsdp")),
        P(("dp", "fsdp")),
        P(("dp", "fsdp"), None),
        P(("dp", "fsdp")),
        P(("dp", "fsdp")),
        P(("dp", "fsdp")),
        P(("dp", "fsdp"), None),
        P(("dp", "fsdp")),
    )
    out_specs = (
        P(("dp", "fsdp"), None),
        P(("dp", "fsdp"), None),
        P(("dp", "fsdp")),
        P(("dp", "fsdp")),
        P(("dp", "fsdp"), None),
        P(("dp", "fsdp")),
        P(("dp", "fsdp")),
        P(("dp", "fsdp")),
        P(("dp", "fsdp"), None),
        P(("dp", "fsdp")),
        P(("dp", "fsdp")),
        P(("dp", "fsdp")),
        P(("dp", "fsdp"), None),
        P(("dp", "fsdp")),
        P(("dp", "fsdp")),
        P(("dp", "fsdp")),
        P(("dp", "fsdp"), None),
        P(("dp", "fsdp")),
    )
    return jax.shard_map(body, mesh=mesh, in_specs=in_specs, out_specs=out_specs, check_vma=False)
```

profile of v0, /device:TPU:0, one launch (start us, length us, event | category | flops | bytes accessed | tf_op | source)
XLA Modules:
  0.0 1078.5 jit_solution(5147558991884384853)
XLA Ops:
  20.2 43.7 %all-reduce.25 = (bf16[1536]{0:T(1024)(128)(2,1)S(1)}, bf16[768]{0:T(1024)(128)(2,1)S(1)}, bf16[768]{0:T(1024)(128)(2,1)S(1)}, bf16[768]{0:T(1024)(128)(2,1)S(1)...) all-reduce(bf16[1536]{0:T(1024)(128)(2,1)S(1)} %dynamic-update-slic, ...), channel_id=1, replica_groups=mesh['dp'=8,'fsdp'=4] {'dp','fsdp'}, use_global_device_ids=true, to_apply=%add.2 | all-reduce | flops 16896 | bytes 67584
  75.6 6.5 add_convert_fusion
  96.1 6.3 convolution_bitcast_fusion
  106.8 6.2 select_reduce_fusion
  117.9 7.8 add_bitcast_fusion
  134.6 60.9 %all-gather.9.cloned.1.call-done = bf16[768,3072]{1,0:T(8,128)(2,1)} async-done(((bf16[24,3072]{1,0:T(8,128)(2,1)}), bf16[768,3072]{1,0:T(8,128)(2,1)}) %all-gather.9.cloned.1.call-update) | async-done | bytes 4718608 | tf_op jit(solution)/shard_map/all_gather | solution.py:227
  200.6 34.1 %fusion.92 = (f32[512]{0:T(512)S(1)}, f32[512,3072]{1,0:T(8,128)}, f32[512,3072]{1,0:T(8,128)}, f32[512]{0:T(512)S(1)}, f32[512,3072]{1,0:T(8,128)}, /*index=5*/f32[512,3072]{1,0:T(8,128)}, f32[512,3072]{1,0:T(8,128)}) fusion(f32[3072]{0:T(1024)S(1)} %convert_element_type.138, f32[512,3072]{1,0:T(8,128)S(1)} %fusion.82, ...), kind=kOutput, calls=%fused_computation.217 | convolution fusion | flops 2625502208 | bytes 44068864 | tf_op jit(solution)/shard_map/dot_general | solution.py:28
  234.7 26.0 %all-gather.11.cloned.1.call-done = bf16[3072,768]{1,0:T(8,128)(2,1)} async-done(((bf16[96,768]{1,0:T(8,128)(2,1)}), bf16[3072,768]{1,0:T(8,128)(2,1)}) %all-gather.11.cloned.1.call-update) | async-done | bytes 4718608 | tf_op jit(solution)/shard_map/all_gather | solution.py:231
  260.8 8.0 fusion.68
  268.8 13.7 %multiply_reduce_fusion.3 = (f32[512]{0:T(512)S(1)}, f32[512]{0:T(512)S(1)}, f32[3072]{0:T(1024)S(1)}, f32[3072]{0:T(1024)S(1)}, f32[512]{0:T(512)S(1)}, /*index=5*/f32[512]{0:T(512)S(1)}, f32[512,3072]{1,0:T(8,128)}) fusion(f32[512,3072]{1,0:T(8,128)} %get-tuple-element.153, f32[3072]{0:T(1024)S(1)} %copy-done.61, f32[512]{0:T(512)S(1)} %broadcast_multiply_fusion.3, ...), kind=kOutput, calls=%fused_computation.30 | convolution fusion | flops 2437931008 | bytes 30720000 | tf_op jit(solution)/shard_map/dot_general | solution.py:38
  282.6 13.0 %multiply_reduce_fusion = (f32[3072]{0:T(1024)S(1)}, f32[512]{0:T(512)S(1)}, f32[512]{0:T(512)S(1)}, f32[3072]{0:T(1024)S(1)}) fusion(f32[512,3072]{1,0:T(8,128)} %fusion.68, f32[512,3072]{1,0:T(8,128)} %get-tuple-element.187, f32[512]{0:T(512)S(1)} %get-tuple-element.196, f32[512]{0:T(512)S(1)} %broadcast_multiply_fusion.2, f32[512]{0:T(512)S(1)} %get-tuple-element.195, ...), kind=kLoop, calls=%fused_computation.23 | loop fusion | flops 31450112 | bytes 25219072 | tf_op jit(solution)/shard_map/transpose(jvp())/reduce_sum | solution.py:20
  295.6 20.2 %convert_reduce_fusion.2 = (f32[3072]{0:T(1024)S(1)}, bf16[512,3072]{1,0:T(8,128)(2,1)}, bf16[512,3072]{1,0:T(8,128)(2,1)}, bf16[512,3072]{1,0:T(8,128)(2,1)}, f32[3072]{0:T(1024)S(1)}, /*index=5*/bf16[512,3072]{1,0:T(8,128)(2,1)}) fusion(f32[512,3072]{1,0:T(8,128)} %get-tuple-element.154, f32[512]{0:T(512)S(1)} %negate_multiply_fusion.7, ...), kind=kLoop, calls=%fused_computation.26 | loop fusion | flops 88074240 | bytes 62992384 | tf_op jit(solution)/shard_map/reduce_sum | solution.py:337
  315.9 5.7 fusion.102
  324.7 7.1 fusion.103
  348.1 7.1 multiply_convert_fusion.1
  355.3 8.7 multiply_convert_fusion
  364.1 9.3 multiply_convert_fusion.2
  376.6 7.4 fusion.45
  384.0 6.7 fusion.31
  397.2 6.2 fusion.36
  407.3 6.1 fusion.101
  430.3 5.2 fusion.84
  435.6 9.8 fusion.77
  450.5 5.3 convolution_add_fusion
  461.2 5.3 convolution_add_fusion.1
  470.7 6.1 add_convert_fusion.10
  476.9 5.0 add_convert_fusion.8
  483.6 71.6 %all-reduce.28.cloned.1.call-done = (f32[768]{0:T(1024)}, f32[768]{0:T(1024)}, f32[1536]{0:T(1024)}, f32[768]{0:T(1024)}, f32[768]{0:T(1024)}, /*index=5*/f32[76...) async-done(((f32[768]{0:T(1024)}, f32[768]{0:T(1024)}, f32[1536]{0:T(1024)}, f32[768]{0:T(1024)}, ...) | async-done | bytes 67600
  570.4 93.5 %reduce-scatter.7.cloned.1.call-done = f32[24,768]{1,0:T(8,128)} async-done(((f32[768,768]{1,0:T(8,128)}), f32[24,768]{1,0:T(8,128)}) %reduce-scatter.7.cloned.1.call-update) | async-done | bytes 73744 | tf_op jit(solution)/shard_map/reduce_scatter | solution.py:399
  663.9 124.4 %reduce-scatter.5.cloned.1.call-done = f32[24,2304]{1,0:T(8,128)} async-done(((f32[768,2304]{1,0:T(8,128)}), f32[24,2304]{1,0:T(8,128)}) %reduce-scatter.5.cloned.1.call-update) | async-done | bytes 221200 | tf_op jit(solution)/shard_map/reduce_scatter | solution.py:395
  788.3 142.2 %reduce-scatter.11.cloned.1.call-done = f32[96,768]{1,0:T(8,128)} async-done(((f32[3072,768]{1,0:T(8,128)}), f32[96,768]{1,0:T(8,128)}) %reduce-scatter.11.cloned.1.call-update) | async-done | bytes 294928 | tf_op jit(solution)/shard_map/reduce_scatter | solution.py:407
  930.6 141.2 %reduce-scatter.9.cloned.1.call-done = f32[24,3072]{1,0:T(8,128)} async-done(((f32[768,3072]{1,0:T(8,128)}), f32[24,3072]{1,0:T(8,128)}) %reduce-scatter.9.cloned.1.call-update) | async-done | bytes 294928 | tf_op jit(solution)/shard_map/reduce_scatter | solution.py:403
  (372 shorter events, 142.2 us)
Async XLA Ops:
  7.2 59.2 %copy-start.94 = (s32[1,8]{1,0:T(1,128)S(1)}, s32[1,8]{1,0:T(1,128)}, u32[]{:S(2)}) copy-start(s32[1,8]{1,0:T(1,128)} %param.20) | copy-start | bytes 100
  7.2 61.0 %copy-start.35 = (bf16[1024,768]{1,0:T(8,128)(2,1)S(1)}, bf16[1024,768]{1,0:T(8,128)(2,1)}, u32[]{:S(2)}) copy-start(bf16[1024,768]{1,0:T(8,128)(2,1)} %param.21) | copy-start | bytes 4718596
  7.2 68.4 %all-gather.5.cloned.1.call-start = ((), (), s32[]{:S(2)}) async-start(), calls=%async_computation.4 | async-start | bytes 3649536 | tf_op jit(solution)/shard_map/all_gather | solution.py:219
  7.9 122.3 %all-gather.7.cloned.1.call-start = ((), (), s32[]{:S(2)}) async-start(), calls=%async_computation.5 | async-start | bytes 1216512 | tf_op jit(solution)/shard_map/all_gather | solution.py:223
  8.7 186.9 %all-gather.9.cloned.1.call-start = ((), (), s32[]{:S(2)}) async-start(), calls=%async_computation.6 | async-start | bytes 4866048 | tf_op jit(solution)/shard_map/all_gather | solution.py:227
  9.4 251.4 %all-gather.11.cloned.1.call-start = ((), (), s32[]{:S(2)}) async-start(), calls=%async_computation.7 | async-start | bytes 4866048 | tf_op jit(solution)/shard_map/all_gather | solution.py:231
  10.0 545.2 %all-reduce.28.cloned.1.call-start = ((), (), s32[]{:S(2)}) async-start(), calls=%async_computation.12 | async-start | bytes 155648
  63.9 11.7 %copy-start.72 = (f32[768]{0:T(1024)}, f32[768]{0:T(1024)S(1)}, u32[]{:S(2)}) copy-start(f32[768]{0:T(1024)S(1)} %convert_element_type.122) | copy-start | bytes 9220
  65.9 16.2 %copy-start.64 = (f32[1024]{0:T(1024)}, f32[1024]{0:T(1024)S(1)}, u32[]{:S(2)}) copy-start(f32[1024]{0:T(1024)S(1)} %broadcast_multiply_fusion.1) | copy-start | bytes 12292
  66.4 15.7 %copy-start.75 = (f32[1024]{0:T(1024)}, f32[1024]{0:T(1024)S(1)}, u32[]{:S(2)}) copy-start(f32[1024]{0:T(1024)S(1)} %fusion.48) | copy-start | bytes 12292
  67.0 60.0 %copy-start.68 = (f32[768]{0:T(1024)}, f32[768]{0:T(1024)S(1)}, u32[]{:S(2)}) copy-start(f32[768]{0:T(1024)S(1)} %convert_element_type.131) | copy-start | bytes 9220
  67.0 133.6 %copy-start.57 = (f32[768]{0:T(1024)}, f32[768]{0:T(1024)S(1)}, u32[]{:S(2)}) copy-start(f32[768]{0:T(1024)S(1)} %convert_element_type.136) | copy-start | bytes 9220
  75.6 37.5 %copy-start.42 = (pred[512,512]{0,1:T(8,128)(4,1)}, pred[512,512]{0,1:T(8,128)(4,1)S(1)}, u32[]{:S(2)}) copy-start(pred[512,512]{0,1:T(8,128)(4,1)S(1)} %get-tuple-element.189) | copy-start | bytes 786436
  85.6 16.9 %copy-start.8 = (bf16[512,768]{0,1:T(8,128)(2,1)}, bf16[512,768]{0,1:T(8,128)(2,1)S(1)}, u32[]{:S(2)}) copy-start(bf16[512,768]{0,1:T(8,128)(2,1)S(1)} %copy.154) | copy-start | bytes 2359300
  102.5 23.5 %copy-start.18 = (f32[512,12,64]{0,2,1:T(8,128)}, f32[512,12,64]{0,2,1:T(8,128)S(1)}, u32[]{:S(2)}) copy-start(f32[512,12,64]{0,2,1:T(8,128)S(1)} %convolution_bitcast_fusion) | copy-start | bytes 4718596
  134.2 66.4 %copy-start.59 = (f32[512]{0:T(512)}, f32[512]{0:T(512)S(1)}, u32[]{:S(2)}) copy-start(f32[512]{0:T(512)S(1)} %broadcast_multiply_fusion.4) | copy-start | bytes 6148
  134.6 66.0 %copy-start.85 = (f32[512]{0:T(512)}, f32[512]{0:T(512)S(1)}, u32[]{:S(2)}) copy-start(f32[512]{0:T(512)S(1)} %get-tuple-element.114) | copy-start | bytes 6148
  134.6 66.0 %copy-start.87 = (f32[512]{0:T(512)}, f32[512]{0:T(512)S(1)}, u32[]{:S(2)}) copy-start(f32[512]{0:T(512)S(1)} %get-tuple-element.115) | copy-start | bytes 6148
  134.6 66.0 %copy-start.66 = (f32[512]{0:T(512)}, f32[512]{0:T(512)S(1)}, u32[]{:S(2)}) copy-start(f32[512]{0:T(512)S(1)} %fusion.52) | copy-start | bytes 6148
  200.6 34.1 %copy-start.10 = (f32[512,3072]{1,0:T(8,128)}, f32[512,3072]{1,0:T(8,128)S(1)}, u32[]{:S(2)}) copy-start(f32[512,3072]{1,0:T(8,128)S(1)} %fusion.82) | copy-start | bytes 18874372
  234.7 34.0 %copy-start.61 = (f32[3072]{0:T(1024)S(1)}, f32[3072]{0:T(1024)}, u32[]{:S(2)}) copy-start(f32[3072]{0:T(1024)} %convert_element_type.139) | copy-start | bytes 36868
  260.8 34.8 %slice-start = ((s8[6291456]{0:T(1024)(128)(4,1)}), s8[4194304]{0:T(1024)(128)(4,1)S(1)}, s32[]{:S(2)}) async-start(s8[6291456]{0:T(1024)(128)(4,1)} %bitcast.105), calls=%async_computation.13 | async-start | bytes 8388608
  268.8 26.8 %slice-start.1 = ((s8[6291456]{0:T(1024)(128)(4,1)}), s8[2097152]{0:T(1024)(128)(4,1)S(1)}, s32[]{:S(2)}) async-start(s8[6291456]{0:T(1024)(128)(4,1)} %bitcast.105), calls=%async_computation.14 | async-start | bytes 4194304
  282.6 13.1 %copy-start.11 = (f32[512,3072]{1,0:T(8,128)S(1)}, f32[512,3072]{1,0:T(8,128)}, u32[]{:S(2)}) copy-start(f32[512,3072]{1,0:T(8,128)} %get-tuple-element.153) | copy-start | bytes 18874372
  282.6 13.1 %copy-start.74 = (f32[3072]{0:T(1024)S(1)}, f32[3072]{0:T(1024)}, u32[]{:S(2)}) copy-start(f32[3072]{0:T(1024)} %convert_element_type.140) | copy-start | bytes 36868
  282.6 33.3 %slice-start.4 = ((s8[4718592]{0:T(1024)(128)(4,1)}), s8[4194304]{0:T(1024)(128)(4,1)S(1)}, s32[]{:S(2)}) async-start(s8[4718592]{0:T(1024)(128)(4,1)} %bitcast.114), calls=%async_computation.17 | async-start | bytes 8388608
  295.6 20.3 %slice-start.5 = ((s8[4718592]{0:T(1024)(128)(4,1)}), s8[524288]{0:T(1024)(128)(4,1)S(1)}, s32[]{:S(2)}) async-start(s8[4718592]{0:T(1024)(128)(4,1)} %bitcast.114), calls=%async_computation.18 | async-start | bytes 1048576
  376.6 15.3 %slice-start.2 = ((s8[6291456]{0:T(1024)(128)(4,1)}), s8[4194304]{0:T(1024)(128)(4,1)S(1)}, s32[]{:S(2)}) async-start(s8[6291456]{0:T(1024)(128)(4,1)} %bitcast.107), calls=%async_computation.15 | async-start | bytes 8388608
  430.2 233.7 %reduce-scatter.7.cloned.1.call-start = ((), (), s32[]{:S(2)}) async-start(), calls=%async_computation.9 | async-start | bytes 2433024 | tf_op jit(solution)/shard_map/reduce_scatter | solution.py:399
  435.5 352.8 %reduce-scatter.5.cloned.1.call-start = ((), (), s32[]{:S(2)}) async-start(), calls=%async_computation.8 | async-start | bytes 7299072 | tf_op jit(solution)/shard_map/reduce_scatter | solution.py:395
  445.4 485.1 %reduce-scatter.11.cloned.1.call-start = ((), (), s32[]{:S(2)}) async-start(), calls=%async_computation.11 | async-start | bytes 9732096 | tf_op jit(solution)/shard_map/reduce_scatter | solution.py:407
  455.9 615.9 %reduce-scatter.9.cloned.1.call-start = ((), (), s32[]{:S(2)}) async-start(), calls=%async_computation.10 | async-start | bytes 9732096 | tf_op jit(solution)/shard_map/reduce_scatter | solution.py:403
  (79 other events, 368.0 us)
Sparse Core Ops, SparseCore 0:
  11.0 63.6 all-gather.4
  77.5 52.5 all-gather.6
  133.1 62.4 all-gather.8
  198.4 62.3 all-gather.10
  430.3 124.8 all-reduce.27
  561.8 102.0 reduce-scatter.6
  670.1 118.1 reduce-scatter.4
  795.8 134.7 reduce-scatter.10
  937.0 134.6 reduce-scatter.8
where the time goes:
time: 1080 us
  waiting for transfers between devices  663 us (61%)
  matrix products  219 us (20%)
  other arithmetic  71.9 us (7%)
  local copies, waits for them, and re-layouts  65.2 us (6%)
  blocking collectives  43.7 us (4%)
  between operations  15.8 us (1%)
    reduce_scatter x1, waiting for transfers between devices, body(): lax.psum_scatter(acc_down_weight, ('dp', 'fsdp'), scatter_dimension=0, ti...  142 us
    reduce_scatter x1, waiting for transfers between devices, body(): lax.psum_scatter(acc_up_weight, ('dp', 'fsdp'), scatter_dimension=0, tile...  141 us
    reduce_scatter x1, waiting for transfers between devices, body(): lax.psum_scatter(acc_qkv_weight, ('dp', 'fsdp'), scatter_dimension=0, til...  124 us
    reduce_scatter x1, waiting for transfers between devices, body(): lax.psum_scatter(acc_out_weight, ('dp', 'fsdp'), scatter_dimension=0, til...  93.5 us
    unnamed x10, waiting for transfers between devices  74.2 us
    all_gather x1, waiting for transfers between devices, body(): lax.all_gather(up_weight, ('dp', 'fsdp'), axis=0, tiled=True)  60.9 us
    dot_general x6, matrix products, product(): return jnp.dot(left, right, preferred_element_type=jnp.float32)  60.3 us
    unnamed x246, local copies, waits for them, and re-layouts  47.1 us
  transfers between devices with their start and end apart: 9, of which 7 were waited for; matrix products, arithmetic and copies ran while one was open for 17% of the time, Pallas kernels for 0%

commit v1 on v0

--- a/solution.py
+++ b/solution.py
@@ -1,8 +1,11 @@
+import functools
 import math
 
 import jax
 import jax.numpy as jnp
 from jax import lax
+from jax.experimental import pallas as pl
+from jax.experimental.pallas import tpu as pltpu
 from jax.sharding import PartitionSpec as P
 
 HD = 64
@@ -41,7 +44,8 @@
 
 
 def segment_ids(lengths, slots):
-    segment_ends = jnp.cumsum(lengths)[:-1]
+    order = jnp.arange(lengths.shape[0], dtype=jnp.int32)
+    segment_ends = jnp.sum(jnp.where(order[None, :] <= order[:, None], lengths[None, :], 0), axis=1)[:-1]
     token_positions = jnp.arange(slots, dtype=jnp.int32)
     return jnp.sum((token_positions[:, None] >= segment_ends[None, :]).astype(jnp.int32), axis=1)
 
@@ -192,7 +196,185 @@
     )
 
 
+AXES = ("dp", "fsdp")
+
+
+def place():
+    outer, inner = lax.axis_index("dp"), lax.axis_index("fsdp")
+    return outer // 2, outer % 2, inner // 2, inner % 2
+
+
+def send(values, dz=0, dx=0, dy=0, dc=0):
+    pairs = []
+    for z in range(4):
+        for x in range(2):
+            for y in range(2):
+                for c in range(2):
+                    here = ((z * 2 + x) * 2 + y) * 2 + c
+                    there = ((((z + dz) % 4) * 2 + (x ^ dx)) * 2 + (y ^ dy)) * 2 + (c ^ dc)
+                    pairs.append((here, there))
+    return lax.ppermute(values, AXES, pairs)
+
+
+def assemble_kernel(spot_ref, *refs):
+    sources, target, sem = refs[:8], refs[8], refs[9]
+    copies = []
+    for part in range(8):
+        for step in range(4):
+            copies.append(
+                pltpu.make_async_copy(
+                    sources[part].at[step],
+                    target.at[spot_ref[part * 4 + step]],
+                    sem.at[part * 4 + step],
+                )
+            )
+    for copy in copies:
+        copy.start()
+    for copy in copies:
+        copy.wait()
+
+
+def assemble(parts):
+    rows, columns = parts[0].shape[1:]
+    z, x, y, c = place()
+    spots = []
+    for part in range(8):
+        dx, dy, dc = part >> 2 & 1, part >> 1 & 1, part & 1
+        for step in range(4):
+            spots.append(((((z - step) % 4) * 2 + (x ^ dx)) * 2 + (y ^ dy)) * 2 + (c ^ dc))
+    whole = pl.pallas_call(
+        assemble_kernel,
+        out_shape=jax.ShapeDtypeStruct((32, rows, columns), parts[0].dtype),
+        in_specs=[pl.BlockSpec(memory_space=pltpu.SMEM)] + [pl.BlockSpec(memory_space=pl.ANY)] * 8,
+        out_specs=pl.BlockSpec(memory_space=pltpu.VMEM),
+        scratch_shapes=[pltpu.SemaphoreType.DMA((32,))],
+        compiler_params=pltpu.CompilerParams(vmem_limit_bytes=16 << 20),
+        cost_estimate=pl.CostEstimate(flops=0, transcendentals=0, bytes_accessed=64 * rows * columns * 2),
+        name="assemble",
+    )(jnp.stack(spots).astype(jnp.int32), *parts)
+    return whole.reshape(32 * rows, columns)
+
+
+def gather(shard, way):
+    near = [shard] + [send(shard, dz=step) for step in (1, 2, 3)]
+    own = jnp.stack(near)
+    across_x, across_y = send(own, dx=1), send(own, dy=1)
+    if way == "x":
+        diagonal = send(across_x, dy=1)
+    elif way == "y":
+        diagonal = send(across_y, dx=1)
+    else:
+        diagonal = send(own, dx=1, dy=1)
+    parts = [own, across_y, across_x, diagonal]
+    both = []
+    for part in parts:
+        both += [part, send(part, dc=1)]
+    return assemble(both)
+
+
+def wide(values):
+    return values.astype(jnp.float32)
+
+
+def scatter_sum(partial, way):
+    rows, columns = partial.shape[0] // 32, partial.shape[1]
+    z, x, y, c = place()
+    view = partial.reshape(4, 2, 2, 2, rows, columns)
+    pick = lax.dynamic_index_in_dim
+    got = send(pick(view, 1 - c, 3, keepdims=False), dc=1)
+    total = (wide(pick(view, c, 3, keepdims=False)) + wide(got)).astype(jnp.bfloat16)
+    if way == "x":
+        got = send(pick(total, 1 - x, 1, keepdims=False), dx=1)
+        total = (wide(pick(total, x, 1, keepdims=False)) + wide(got)).astype(jnp.bfloat16)
+        got = send(pick(total, 1 - y, 1, keepdims=False), dy=1)
+        total = (wide(pick(total, y, 1, keepdims=False)) + wide(got)).astype(jnp.bfloat16)
+    else:
+        got = send(pick(total, 1 - y, 2, keepdims=False), dy=1)
+        total = (wide(pick(total, y, 2, keepdims=False)) + wide(got)).astype(jnp.bfloat16)
+        got = send(pick(total, 1 - x, 1, keepdims=False), dx=1)
+        total = (wide(pick(total, x, 1, keepdims=False)) + wide(got)).astype(jnp.bfloat16)
+    result = wide(pick(total, z, 0, keepdims=False))
+    for step in (1, 2, 3):
+        result = result + wide(send(pick(total, (z + step) % 4, 0, keepdims=False), dz=step))
+    return result
+
+
+def gather_vectors(shards):
+    sizes = [shard.shape[0] for shard in shards]
+    packed = jnp.concatenate(shards)
+    count = packed.shape[0]
+    packed = jnp.pad(packed, (0, -count % 128)).reshape(1, -1)
+    z, x, y, c = place()
+    first = [packed] + [
+        lax.ppermute(packed, "fsdp", [(i, i ^ flip) for i in range(4)]) for flip in (1, 2, 3)
+    ]
+    inner = lax.axis_index("fsdp")
+    ranked = jnp.stack([_choose(first, inner ^ spot) for spot in range(4)])
+    outer = lax.axis_index("dp")
+    second = [ranked] + [
+        lax.ppermute(ranked, "dp", [(i, i ^ flip) for i in range(8)]) for flip in range(1, 8)
+    ]
+    everything = jnp.stack([_choose(second, outer ^ spot) for spot in range(8)]).reshape(32, -1)
+    full, start = [], 0
+    for size in sizes:
+        full.append(everything[:, start : start + size].reshape(-1))
+        start += size
+    return full
+
+
+def _choose(options, index):
+    picked = options[0]
+    for number, option in enumerate(options[1:], 1):
+        picked = jnp.where(index == number, option, picked)
+    return picked
+
+
+def sum_vectors(vectors):
+    sizes = [vector.shape[0] for vector in vectors]
+    packed = jnp.concatenate(vectors).reshape(-1, 128)
+    for flip in (1, 2):
+        packed = packed + lax.ppermute(packed, "fsdp", [(i, i ^ flip) for i in range(4)])
+    for flip in (1, 2, 4):
+        packed = packed + lax.ppermute(packed, "dp", [(i, i ^ flip) for i in range(8)])
+    flat = packed.reshape(-1)
+    here = lax.axis_index("dp") * 4 + lax.axis_index("fsdp")
+    out, start = [], 0
+    for size in sizes:
+        out.append(lax.dynamic_slice(flat, (start + here * (size // 32),), (size // 32,)))
+        start += size
+    return out
+
+
+def gather_all(staged, shards):
+    if not staged:
+        return [lax.all_gather(shard, AXES, axis=0, tiled=True) for shard in shards]
+    full = [None] * 16
+    small = [index for index in range(16) if index not in (2, 6, 10, 14)]
+    for index, whole in zip(small, gather_vectors([shards[index] for index in small])):
+        full[index] = whole
+    full[2] = gather(shards[2], "both")
+    full[6] = gather(shards[6], "both")
+    full[10] = gather(shards[10], "x")
+    full[14] = gather(shards[14], "y")
+    return full
+
+
+def sum_all(staged, parts):
+    if not staged:
+        return [lax.psum_scatter(part, AXES, scatter_dimension=0, tiled=True) for part in parts]
+    out = [None] * 16
+    last = [0, 1, 3]
+    early = [index for index in range(16) if index not in (2, 6, 10, 14) and index not in last]
+    for group in (early, last):
+        for index, total in zip(group, sum_vectors([parts[index] for index in group])):
+            out[index] = total
+    for index, way in ((14, "x"), (10, "y"), (6, "x"), (2, "y")):
+        out[index] = scatter_sum(parts[index].astype(jnp.bfloat16), way)
+    return out
+
+
 def body(
+    staged,
     tokens,
     seg_lengths,
     cotangent,
@@ -213,24 +395,9 @@
     down_weight,
     down_bias,
 ):
-    gathered = (
-        lax.all_gather(in_gain, ("dp", "fsdp"), axis=0, tiled=True),
-        lax.all_gather(in_bias, ("dp", "fsdp"), axis=0, tiled=True),
-        lax.all_gather(qkv_weight, ("dp", "fsdp"), axis=0, tiled=True),
-        lax.all_gather(qv_bias, ("dp", "fsdp"), axis=0, tiled=True),
-        lax.all_gather(mid_gain, ("dp", "fsdp"), axis=0, tiled=True),
-        lax.all_gather(mid_bias, ("dp", "fsdp"), axis=0, tiled=True),
-        lax.all_gather(out_weight, ("dp", "fsdp"), axis=0, tiled=True),
-        lax.all_gather(out_bias, ("dp", "fsdp"), axis=0, tiled=True),
-        lax.all_gather(ffn_gain, ("dp", "fsdp"), axis=0, tiled=True),
-        lax.all_gather(ffn_bias, ("dp", "fsdp"), axis=0, tiled=True),
-        lax.all_gather(up_weight, ("dp", "fsdp"), axis=0, tiled=True),
-        lax.all_gather(up_bias, ("dp", "fsdp"), axis=0, tiled=True),
-        lax.all_gather(hid_gain, ("dp", "fsdp"), axis=0, tiled=True),
-        lax.all_gather(hid_bias, ("dp", "fsdp"), axis=0, tiled=True),
-        lax.all_gather(down_weight, ("dp", "fsdp"), axis=0, tiled=True),
-        lax.all_gather(down_bias, ("dp", "fsdp"), axis=0, tiled=True),
-    )
+    gathered = gather_all(staged, (
+        in_gain, in_bias, qkv_weight, qv_bias, mid_gain, mid_bias, out_weight, out_bias, ffn_gain, ffn_bias, up_weight, up_bias, hid_gain, hid_bias, down_weight, down_bias
+    ))
     model_width = tokens.shape[1]
     head_count = model_width // HD
     block_count = ROW // BLOCK
@@ -293,24 +460,7 @@
             ffn_kept,
         )
     ]
-    weights_back = (
-        lax.all_gather(in_gain, ("dp", "fsdp"), axis=0, tiled=True),
-        lax.all_gather(in_bias, ("dp", "fsdp"), axis=0, tiled=True),
-        lax.all_gather(qkv_weight, ("dp", "fsdp"), axis=0, tiled=True),
-        lax.all_gather(qv_bias, ("dp", "fsdp"), axis=0, tiled=True),
-        lax.all_gather(mid_gain, ("dp", "fsdp"), axis=0, tiled=True),
-        lax.all_gather(mid_bias, ("dp", "fsdp"), axis=0, tiled=True),
-        lax.all_gather(out_weight, ("dp", "fsdp"), axis=0, tiled=True),
-        lax.all_gather(out_bias, ("dp", "fsdp"), axis=0, tiled=True),
-        lax.all_gather(ffn_gain, ("dp", "fsdp"), axis=0, tiled=True),
-        lax.all_gather(ffn_bias, ("dp", "fsdp"), axis=0, tiled=True),
-        lax.all_gather(up_weight, ("dp", "fsdp"), axis=0, tiled=True),
-        lax.all_gather(up_bias, ("dp", "fsdp"), axis=0, tiled=True),
-        lax.all_gather(hid_gain, ("dp", "fsdp"), axis=0, tiled=True),
-        lax.all_gather(hid_bias, ("dp", "fsdp"), axis=0, tiled=True),
-        lax.all_gather(down_weight, ("dp", "fsdp"), axis=0, tiled=True),
-        lax.all_gather(down_bias, ("dp", "fsdp"), axis=0, tiled=True),
-    )
+    weights_back = gathered
     acc_ffn_gain = jnp.zeros(ffn_gain_full.shape, jnp.float32)
     acc_ffn_bias = jnp.zeros(ffn_gain_full.shape, jnp.float32)
     acc_up_weight = jnp.zeros(gathered[10].shape, jnp.float32)
@@ -389,24 +539,9 @@
     grad_one = product_nt(grad_projected, weights_back[2])
     grad_input_part, part_gain, part_bias = in_back(grad_one)
     grad_rows = grad_middle + grad_input_part
-    summed = (
-        lax.psum_scatter(part_gain, ("dp", "fsdp"), scatter_dimension=0, tiled=True),
-        lax.psum_scatter(part_bias, ("dp", "fsdp"), scatter_dimension=0, tiled=True),
-        lax.psum_scatter(acc_qkv_weight, ("dp", "fsdp"), scatter_dimension=0, tiled=True),
-        lax.psum_scatter(acc_qv_bias, ("dp", "fsdp"), scatter_dimension=0, tiled=True),
-        lax.psum_scatter(acc_mid_gain, ("dp", "fsdp"), scatter_dimension=0, tiled=True),
-        lax.psum_scatter(acc_mid_bias, ("dp", "fsdp"), scatter_dimension=0, tiled=True),
-        lax.psum_scatter(acc_out_weight, ("dp", "fsdp"), scatter_dimension=0, tiled=True),
-        lax.psum_scatter(acc_out_bias, ("dp", "fsdp"), scatter_dimension=0, tiled=True),
-        lax.psum_scatter(acc_ffn_gain, ("dp", "fsdp"), scatter_dimension=0, tiled=True),
-        lax.psum_scatter(acc_ffn_bias, ("dp", "fsdp"), scatter_dimension=0, tiled=True),
-        lax.psum_scatter(acc_up_weight, ("dp", "fsdp"), scatter_dimension=0, tiled=True),
-        lax.psum_scatter(acc_up_bias, ("dp", "fsdp"), scatter_dimension=0, tiled=True),
-        lax.psum_scatter(acc_hid_gain, ("dp", "fsdp"), scatter_dimension=0, tiled=True),
-        lax.psum_scatter(acc_hid_bias, ("dp", "fsdp"), scatter_dimension=0, tiled=True),
-        lax.psum_scatter(acc_down_weight, ("dp", "fsdp"), scatter_dimension=0, tiled=True),
-        lax.psum_scatter(acc_down_bias, ("dp", "fsdp"), scatter_dimension=0, tiled=True),
-    )
+    summed = sum_all(staged, (
+        part_gain, part_bias, acc_qkv_weight, acc_qv_bias, acc_mid_gain, acc_mid_bias, acc_out_weight, acc_out_bias, acc_ffn_gain, acc_ffn_bias, acc_up_weight, acc_up_bias, acc_hid_gain, acc_hid_bias, acc_down_weight, acc_down_bias
+    ))
     return (
         out_rows,
         grad_rows,
@@ -471,4 +606,5 @@
         P(("dp", "fsdp"), None),
         P(("dp", "fsdp")),
     )
-    return jax.shard_map(body, mesh=mesh, in_specs=in_specs, out_specs=out_specs, check_vma=False)
+    staged = (mesh.shape["dp"], mesh.shape["fsdp"]) == (8, 4)
+    return jax.shard_map(functools.partial(body, staged), mesh=mesh, in_specs=in_specs, out_specs=out_specs, check_vma=False)

time: 1080 us -> 600 us (0.56)
  waiting for transfers between devices: 663 us -> 119 us
  starting transfers between devices: 0.57 us -> 79.1 us
  blocking collectives: 43.7 us -> 0 us
  local copies, waits for them, and re-layouts: 65.2 us -> 85.8 us
  Pallas kernels: 0 us -> 17.6 us
  matrix products: 219 us -> 204 us
  other arithmetic: 71.9 us -> 84.9 us
  between operations: 15.8 us -> 3.28 us
    reduce_scatter x4 -> x0, waiting for transfers between devices: 501 us -> none  [the longest x1 142 us: body(): lax.psum_scatter(acc_down_weight, ('dp', 'fsdp'), scatter_dimension=0, ti...]
    ppermute x0 -> x84, waiting for transfers between devices: none -> 119 us  [the longest x64 108 us: send(): return lax.ppermute(values, AXES, pairs)]
    all_gather x4 -> x0, waiting for transfers between devices: 87 us -> none  [the longest x1 60.9 us: body(): lax.all_gather(up_weight, ('dp', 'fsdp'), axis=0, tiled=True)]
    ppermute x0 -> x84, starting transfers between devices: none -> 79.1 us  [the longest x64 55.9 us: send(): return lax.ppermute(values, AXES, pairs)]
    unnamed x10 -> x0, waiting for transfers between devices: 74.2 us -> none
    unnamed x1 -> x0, blocking collectives: 43.7 us -> none
    unnamed x246 -> x319, local copies, waits for them, and re-layouts: 47.1 us -> 27.8 us
    pallas_call x0 -> x4, Pallas kernels: none -> 17.6 us  [assemble(): pl.pallas_call(assemble_kernel, out_shape=jax.ShapeDtypeStruct((32, rows,...]
  transfers between devices with their start and end apart: 9 -> 84, of which waited for: 7 -> 29; matrix products, arithmetic and copies ran while one was open for 17% -> 28% of each run, Pallas kernels for 0% -> 2%
where the time goes in v1:
time: 600 us; the launch traced here: 594 us
  matrix products  204 us (34%)
  waiting for transfers between devices  119 us (20%)
  local copies, waits for them, and re-layouts  85.8 us (14%)
  other arithmetic  84.9 us (14%)
  starting transfers between devices  79.1 us (13%)
  Pallas kernels  17.6 us (3%)
    ppermute x64, waiting for transfers between devices, send(): return lax.ppermute(values, AXES, pairs)  108 us
    ppermute x64, starting transfers between devices, send(): return lax.ppermute(values, AXES, pairs)  55.9 us
    dot_general x6, matrix products, product(): return jnp.dot(left, right, preferred_element_type=jnp.float32)  50.5 us
    dot_general x6, matrix products, product_nt(): lax.dot_general(left, right, (((1,), (1,)), ((), ())), preferred_element_...  32.2 us
    dot_general x6, matrix products, product_tn(): lax.dot_general(left, right, (((0,), (0,)), ((), ())), preferred_element_...  31.1 us
    unnamed x319, local copies, waits for them, and re-layouts  27.8 us
    dot_general x3, matrix products, attend_backward(): jnp.einsum('qhd,khd->hqk', grad_block, value_tile_rows, preferred_element...  27.8 us
    reduce_sum x8, other arithmetic, layer_norm(): return center * lax.rsqrt(spread + EPSILON) * norm_gain + norm_bias  22.6 us
  transfers between devices with their start and end apart: 84, of which 29 were waited for; matrix products, arithmetic and copies ran while one was open for 28% of the time, Pallas kernels for 2%

profile of v1, /device:TPU:0, one launch (start us, length us, event | category | flops | bytes accessed | tf_op | source)
XLA Modules:
  0.0 593.9 jit_solution(17249462182198235301)
XLA Ops:
  0.7 8.1 %concatenate.50 = bf16[528]{0:T(1024)(128)(2,1)S(1)} concatenate(bf16[24]{0:T(256)(128)(2,1)} %param.22, bf16[24]{0:T(256)(128)(2,1)} %param.23, bf16[48]{0:T(256)(128)(2,1)} %param.25, bf16[24]{0:T(256)(128)(2,1)} %param.26, bf16[24]{0:T(256)(128)(2,1)} %param.27, bf16[24]{0:T(256)(128)(2,1)} %param.29, bf16[24]{0:T(256)(128)(2,1)} %param.30, bf16[24]{0:T(256)(128)(2,1)} %param.31, ...), dimensions={0} | concatenate | bytes 2112 | tf_op jit(solution)/shard_map/concatenate | solution.py:304
  40.3 5.1 collective-permute-done.20
  59.2 7.4 %collective-permute-done.31 = bf16[24,3072]{1,0:T(8,128)(2,1)S(1)} collective-permute-done((bf16[24,3072]{1,0:T(8,128)(2,1)S(1)}, bf16[24,3072]{1,0:T(8,128)(2,1)S(1)}, u32[]{:S(2)}, u32[]{:S(2)}) %collective-permute-start.31) | collective-permute-done | bytes 147488 | tf_op jit(solution)/shard_map/ppermute | solution.py:216
  89.3 9.5 %collective-permute-done.18.refs_6_ = bf16[4,24,2304]{2,1,0:T(8,128)(2,1)} collective-permute-done((bf16[4,24,2304]{2,1,0:T(8,128)(2,1)S(1)}, bf16[4,24,2304]{2,1,0:T(8,128)(2,1)}, u32[]{:S(2)}, u32[]{:S(2)}) %collective-permute-start.18) | collective-permute-done | bytes 442400 | tf_op jit(solution)/shard_map/ppermute | solution.py:216
  148.0 8.6 %fusion.78 = f32[12,64,512]{2,1,0:T(8,128)} fusion(bf16[512,12,64]{0,2,1:T(8,128)(2,1)} %bitcast.392, f32[12,512,512]{1,2,0:T(8,128)} %copy-done.28, f32[12,512]{1,0:T(8,128)S(1)} %copy-done.118, pred[512,512]{0,1:T(8,128)(4,1)S(1)} %copy-done.70), kind=kOutput, calls=%fused_computation.240 | convolution fusion | flops 415236096 | bytes 15228928 | tf_op jit(solution)/shard_map/hqk,khd->qhd/dot_general | solution.py:117
  160.9 6.3 %select_reduce_fusion = (f32[12,512]{1,0:T(8,128)S(1)}, f32[12,512]{1,0:T(8,128)S(1)}) fusion(f32[12,512,512]{1,2,0:T(8,128)S(1)} %get-tuple-element.204, f32[12,512]{1,0:T(8,128)S(1)} %get-tuple-element.178, pred[512,512]{0,1:T(8,128)(4,1)S(1)} %copy-done.68, f32[12,512]{1,0:T(8,128)S(1)} %get-tuple-element.177, f32[12,512,512]{1,2,0:T(8,128)S(1)} %get-tuple-element.202, ...), kind=kLoop, calls=%fused_computation.5 | loop fusion | flops 31444992 | bytes 25788416 | tf_op jit(solution)/shard_map/reduce_sum | solution.py:99
  173.4 7.9 %convolution_add_fusion = f32[12,64,512]{2,1,0:T(8,128)S(1)} fusion(f32[12,64,512]{2,1,0:T(8,128)} %fusion.74, bf16[512,12,64]{0,2,1:T(8,128)(2,1)} %bitcast.396, f32[12,512,512]{1,2,0:T(8,128)} %copy-done.29, f32[12,512]{1,0:T(8,128)} %copy-done.120, pred[512,512]{0,1:T(8,128)(4,1)S(1)} %copy-done.68), kind=kOutput, calls=%fused_computation.156 | convolution fusion | flops 415629312 | bytes 16801792 | tf_op jit(solution)/shard_map/hqk,khd->qhd/dot_general | solution.py:117
  190.2 12.9 %collective-permute-done.48.refs_6_ = bf16[4,96,768]{2,1,0:T(8,128)(2,1)S(1)} collective-permute-done((bf16[4,96,768]{2,1,0:T(8,128)(2,1)}, bf16[4,96,768]{2,1,0:T(8,128)(2,1)S(1)}, u32[]{:S(2)}, u32[]{:S(2)}) %collective-permute-start.48) | collective-permute-done | bytes 589856 | tf_op jit(solution)/shard_map/ppermute | solution.py:216
  203.1 5.5 assemble.6
  211.6 34.1 %fusion.127 = (f32[512]{0:T(512)S(1)}, f32[512,3072]{1,0:T(8,128)}, f32[512,3072]{1,0:T(8,128)}, f32[512]{0:T(512)S(1)}, f32[512,3072]{1,0:T(8,128)}, /*index=5*/f32[512,3072]{1,0:T(8,128)}, f32[512,3072]{1,0:T(8,128)}) fusion(f32[3072]{0:T(1024)S(1)} %copy-done.102, f32[512,3072]{1,0:T(8,128)S(1)} %fusion.118, bf16[768,3072]{1,0:T(8,128)(2,1)S(1)} %bitcast.334, ...), kind=kOutput, calls=%fused_computation.359 | convolution fusion | flops 2625502208 | bytes 44068864 | tf_op jit(solution)/shard_map/dot_general | solution.py:31
  245.8 6.1 %assemble.7 = bf16[32,96,768]{2,1,0:T(8,128)(2,1)S(1)} custom-call(s32[32]{0:T(128)S(1)} %stack.346.spot_ref, bf16[4,96,768]{2,1,0:T(8,128)(2,1)S(1)} %pad_maximum_fusion.8.refs_0_, bf16[4,96,768]{2,1,0:T(8,128)(2,1)S(1)} %collective-permute-done.43.refs_1_, bf16[4,96,768]{2,1,0:T(8,128)(2,1)} %collective-permute-done.44.refs_2_, ...), custom_call_target="tpu_custom_call" | custom-call | bytes 9437184 | tf_op jit(solution)/shard_map/assemble/pallas_call | solution.py:245
  252.0 5.2 multiply_reduce_fusion.1
  257.2 10.3 %fusion.6 = (f32[3072]{0:T(1024)}, f32[512]{0:T(512)S(1)}, f32[512]{0:T(512)S(1)}, f32[512]{0:T(512)S(1)}, f32[3072,512]{0,1:T(8,128)S(1)}) fusion(f32[3072,512]{0,1:T(8,128)} %get-tuple-element.208, f32[512,3072]{1,0:T(8,128)} %get-tuple-element.108, f32[512]{0:T(512)S(1)} %get-tuple-element.199, f32[512]{0:T(512)S(1)} %broadcast_multiply_fusion.3, ...), kind=kOutput, calls=%fused_computation.30 | convolution fusion | flops 2441080320 | bytes 30709760 | tf_op jit(solution)/shard_map/dot_general | solution.py:41
  267.5 7.5 %fusion.5 = (f32[3072]{0:T(1024)}, f32[512]{0:T(512)S(1)}) fusion(f32[3072,512]{0,1:T(8,128)S(1)} %get-tuple-element.209, f32[512,3072]{1,0:T(8,128)} %get-tuple-element.186, f32[512]{0:T(512)S(1)} %get-tuple-element.197, f32[512]{0:T(512)S(1)} %broadcast_multiply_fusion.2, f32[512]{0:T(512)S(1)} %get-tuple-element.196, f32[3072]{0:T(1024)S(1)} %copy-done.90), kind=kLoop, calls=%fused_computation.27 | loop fusion | flops 15725056 | bytes 12615680 | tf_op jit(solution)/shard_map/transpose(jvp())/reduce_sum | solution.py:23
  275.1 21.0 %convert_reduce_fusion.2 = (f32[3072]{0:T(1024)}, bf16[512,3072]{1,0:T(8,128)(2,1)}, bf16[512,3072]{1,0:T(8,128)(2,1)}, bf16[512,3072]{1,0:T(8,128)(2,1)}, f32[3072]{0:T(1024)}, /*index=5*/bf16[512,3072]{1,0:T(8,128)(2,1)}) fusion(f32[512,3072]{1,0:T(8,128)} %get-tuple-element.109, f32[512]{0:T(512)S(1)} %negate_multiply_fusion.7, ...), kind=kLoop, calls=%fused_computation.32 | loop fusion | flops 88074240 | bytes 62992384 | tf_op jit(solution)/shard_map/reduce_sum | solution.py:487
  296.1 7.7 %fusion.116 = f32[768,3072]{1,0:T(8,128)} fusion(bf16[512,3072]{1,0:T(8,128)(2,1)} %get-tuple-element.103, f32[1024,768]{0,1:T(8,128)S(1)} %fusion.31, f32[768]{0:T(1024)S(1)} %reshape.680, f32[768]{0:T(1024)S(1)} %reshape.679, f32[512]{0:T(512)S(1)} %fusion.86, f32[512]{0:T(512)S(1)} %broadcast_multiply_fusion.5), kind=kOutput, calls=%fused_computation.351 | convolution fusion | flops 2417885184 | bytes 14168064 | tf_op jit(solution)/shard_map/dot_general | solution.py:35
  335.3 8.4 %multiply_convert_fusion.1 = bf16[12,512,512]{1,2,0:T(8,128)(2,1)} fusion(f32[12,512,512]{1,2,0:T(8,128)S(1)} %bitcast.350, f32[12,512]{1,0:T(8,128)S(1)} %get-tuple-element.153, f32[12,512]{1,0:T(8,128)S(1)} %copy-done.121, pred[512,512]{0,1:T(8,128)(4,1)S(1)} %copy-done.67, bf16[512,12,64]{0,2,1:T(8,128)(2,1)} %bitcast.398, bf16[512,12,64]{0,2,1:T(8,128)(2,1)} %bitcast.393), kind=kOutput, calls=%fused_computation.1 | convolution fusion | flops 421527552 | bytes 20758528 | tf_op jit(solution)/shard_map/qhd,khd->hqk/dot_general | solution.py:174
  343.8 12.0 %multiply_convert_fusion = bf16[12,512,512]{1,2,0:T(8,128)(2,1)} fusion(f32[12,512,512]{1,2,0:T(8,128)} %copy-done.29, f32[12,512]{1,0:T(8,128)S(1)} %get-tuple-element.153, f32[12,512]{1,0:T(8,128)S(1)} %copy-done.121, pred[512,512]{0,1:T(8,128)(4,1)S(1)} %copy-done.69, bf16[512,12,64]{0,2,1:T(8,128)(2,1)} %bitcast.399, bf16[512,12,64]{0,2,1:T(8,128)(2,1)} %bitcast.397), kind=kOutput, calls=%fused_computation | convolution fusion | flops 421527552 | bytes 20758528 | tf_op jit(solution)/shard_map/qhd,khd->hqk/dot_general | solution.py:174
  355.8 7.3 %multiply_convert_fusion.2 = bf16[12,512,512]{1,2,0:T(8,128)(2,1)S(1)} fusion(f32[12,512,512]{1,2,0:T(8,128)} %copy-done.28, f32[12,512]{1,0:T(8,128)S(1)} %get-tuple-element.152, f32[12,512]{1,0:T(8,128)S(1)} %copy-done.119, pred[512,512]{0,1:T(8,128)(4,1)S(1)} %copy-done.71, bf16[512,12,64]{0,2,1:T(8,128)(2,1)S(1)} %bitcast.402, ...), kind=kOutput, calls=%fused_computation.2 | convolution fusion | flops 421527552 | bytes 20758528 | tf_op jit(solution)/shard_map/qhd,khd->hqk/dot_general | solution.py:174
  368.4 7.3 %fusion.76 = f32[12,64,512]{2,1,0:T(8,128)} fusion(bf16[512,12,64]{0,2,1:T(8,128)(2,1)S(1)} %bitcast.403, f32[12,512,512]{1,2,0:T(8,128)} %copy-done.28, f32[12,512]{1,0:T(8,128)S(1)} %copy-done.119, pred[512,512]{0,1:T(8,128)(4,1)S(1)} %copy-done.71), kind=kOutput, calls=%fused_computation.239 | convolution fusion | flops 415236096 | bytes 15228928 | tf_op jit(solution)/shard_map/hqk,qhd->khd/dot_general | solution.py:168
  390.1 5.2 fusion.52
  407.0 5.6 fusion.138
  412.6 6.0 %convolution_convert_fusion = bf16[768,2304]{1,0:T(8,128)(2,1)} fusion(bf16[1024,768]{0,1:T(8,128)(2,1)S(1)} %copy-done.25, f32[768]{0:T(1024)S(1)} %copy-done.132, f32[768]{0:T(1024)S(1)} %copy-done.99, f32[1024]{0:T(1024)S(1)} %copy-done.110, f32[1024]{0:T(1024)S(1)} %copy-done.93, bf16[1024,768]{0,1:T(8,128)(2,1)S(1)} %bitcast.385, ...), kind=kOutput, calls=%fused_computation.69 | convolution fusion | flops 3644522496 | bytes 9844736 | tf_op jit(solution)/shard_map/dot_general | solution.py:35
  421.0 5.3 fusion.107
  433.4 5.3 add_convert_fusion
  443.2 5.4 add_convert_fusion.1
  518.0 11.9 %collective-permute-done.56 = bf16[4,2,24,2304]{3,2,0,1:T(8,128)(2,1)S(1)} collective-permute-done((bf16[4,2,24,2304]{3,2,0,1:T(8,128)(2,1)S(1)}, bf16[4,2,24,2304]{3,2,0,1:T(8,128)(2,1)S(1)}, u32[]{:S(2)}, u32[]{:S(2)}) %collective-permute-start.56) | collective-permute-done | bytes 884768 | tf_op jit(solution)/shard_map/ppermute | solution.py:216
  535.1 15.4 %collective-permute-done.57 = bf16[4,24,2304]{2,1,0:T(8,128)(2,1)S(1)} collective-permute-done((bf16[4,24,2304]{2,1,0:T(8,128)(2,1)S(1)}, bf16[4,24,2304]{2,1,0:T(8,128)(2,1)S(1)}, u32[]{:S(2)}, u32[]{:S(2)}) %collective-permute-start.57) | collective-permute-done | bytes 442400 | tf_op jit(solution)/shard_map/ppermute | solution.py:216
  555.8 5.5 collective-permute-done.73
  563.9 5.5 collective-permute-done.80
  579.0 4.9 collective-permute-done.82
  585.6 7.3 %collective-permute-done.76 = bf16[24,3072]{1,0:T(8,128)(2,1)S(1)} collective-permute-done((bf16[24,3072]{1,0:T(8,128)(2,1)S(1)}, bf16[24,3072]{1,0:T(8,128)(2,1)S(1)}, u32[]{:S(2)}, u32[]{:S(2)}) %collective-permute-start.76) | collective-permute-done | bytes 147488 | tf_op jit(solution)/shard_map/ppermute | solution.py:216
  (667 shorter events, 309.2 us)
Async XLA Ops:
  33.5 19.6 %collective-permute-start.10 = (bf16[24,2304]{1,0:T(8,128)(2,1)S(1)}, bf16[24,2304]{1,0:T(8,128)(2,1)S(1)}, u32[]{:S(2)}, u32[]{:S(2)}) collective-permute-start(bf16[24,2304]{1,0:T(8,128)(2,1)S(1)} %copy-done.91), channel_id=1, source_target_pairs={{0,8},{1,9},{2,10},{3,11},{4,12},{5,13},{6,14},{7,15},{8,16},{9,17... | collective-permute-start | bytes 331784 | tf_op jit(solution)/shard_map/ppermute | solution.py:216
  34.9 18.9 %collective-permute-start.11 = (bf16[24,2304]{1,0:T(8,128)(2,1)S(1)}, bf16[24,2304]{1,0:T(8,128)(2,1)S(1)}, u32[]{:S(2)}, u32[]{:S(2)}) collective-permute-start(bf16[24,2304]{1,0:T(8,128)(2,1)S(1)} %copy-done.91), channel_id=1, source_target_pairs={{0,16},{1,17},{2,18},{3,19},{4,20},{5,21},{6,22},{7,23},{8,24},{9,... | collective-permute-start | bytes 331784 | tf_op jit(solution)/shard_map/ppermute | solution.py:216
  37.8 17.3 %collective-permute-start.12 = (bf16[24,2304]{1,0:T(8,128)(2,1)S(1)}, bf16[24,2304]{1,0:T(8,128)(2,1)S(1)}, u32[]{:S(2)}, u32[]{:S(2)}) collective-permute-start(bf16[24,2304]{1,0:T(8,128)(2,1)S(1)} %copy-done.91), channel_id=1, source_target_pairs={{0,24},{1,25},{2,26},{3,27},{4,28},{5,29},{6,30},{7,31},{8,0},{9,1... | collective-permute-start | bytes 331784 | tf_op jit(solution)/shard_map/ppermute | solution.py:216
  49.3 17.3 %collective-permute-start.31 = (bf16[24,3072]{1,0:T(8,128)(2,1)S(1)}, bf16[24,3072]{1,0:T(8,128)(2,1)S(1)}, u32[]{:S(2)}, u32[]{:S(2)}) collective-permute-start(bf16[24,3072]{1,0:T(8,128)(2,1)S(1)} %copy-done.87), channel_id=1, source_target_pairs={{0,16},{1,17},{2,18},{3,19},{4,20},{5,21},{6,22},{7,23},{8,24},{9,... | collective-permute-start | bytes 442376 | tf_op jit(solution)/shard_map/ppermute | solution.py:216
  53.8 15.4 %collective-permute-start.40 = (bf16[96,768]{1,0:T(8,128)(2,1)S(1)}, bf16[96,768]{1,0:T(8,128)(2,1)S(1)}, u32[]{:S(2)}, u32[]{:S(2)}) collective-permute-start(bf16[96,768]{1,0:T(8,128)(2,1)S(1)} %copy-done.88), channel_id=1, source_target_pairs={{0,8},{1,9},{2,10},{3,11},{4,12},{5,13},{6,14},{7,15},{8,16},{9,17... | collective-permute-start | bytes 442376 | tf_op jit(solution)/shard_map/ppermute | solution.py:216
  55.1 19.5 %collective-permute-start.41 = (bf16[96,768]{1,0:T(8,128)(2,1)S(1)}, bf16[96,768]{1,0:T(8,128)(2,1)S(1)}, u32[]{:S(2)}, u32[]{:S(2)}) collective-permute-start(bf16[96,768]{1,0:T(8,128)(2,1)S(1)} %copy-done.88), channel_id=1, source_target_pairs={{0,16},{1,17},{2,18},{3,19},{4,20},{5,21},{6,22},{7,23},{8,24},{9,... | collective-permute-start | bytes 442376 | tf_op jit(solution)/shard_map/ppermute | solution.py:216
  57.4 17.3 %collective-permute-start.42 = (bf16[96,768]{1,0:T(8,128)(2,1)S(1)}, bf16[96,768]{1,0:T(8,128)(2,1)S(1)}, u32[]{:S(2)}, u32[]{:S(2)}) collective-permute-start(bf16[96,768]{1,0:T(8,128)(2,1)S(1)} %copy-done.88), channel_id=1, source_target_pairs={{0,24},{1,25},{2,26},{3,27},{4,28},{5,29},{6,30},{7,31},{8,0},{9,1... | collective-permute-start | bytes 442376 | tf_op jit(solution)/shard_map/ppermute | solution.py:216
  77.5 21.3 %collective-permute-start.18 = (bf16[4,24,2304]{2,1,0:T(8,128)(2,1)S(1)}, bf16[4,24,2304]{2,1,0:T(8,128)(2,1)}, u32[]{:S(2)}, u32[]{:S(2)}) collective-permute-start(bf16[4,24,2304]{2,1,0:T(8,128)(2,1)S(1)} %pad_maximum_fusion.9.refs_0_), channel_id=1, source_target_pairs={{0,6},{1,7},{2,4},{3,5},{4,2},{5,3},{6,0},{7,1},{8,14},{9,15},{10,... | collective-permute-start | bytes 1327112 | tf_op jit(solution)/shard_map/ppermute | solution.py:216
  79.7 34.3 %collective-permute-start.36 = (bf16[4,24,3072]{2,1,0:T(8,128)(2,1)S(1)}, bf16[4,24,3072]{2,1,0:T(8,128)(2,1)S(1)}, u32[]{:S(2)}, u32[]{:S(2)}) collective-permute-start(bf16[4,24,3072]{2,1,0:T(8,128)(2,1)S(1)} %pad_maximum_fusion.7.refs_0_), channel_id=1, source_target_pairs={{0,4},{1,5},{2,6},{3,7},{4,0},{5,1},{6,2},{7,3},{8,12},{9,13},{10,... | collective-permute-start | bytes 1769480 | tf_op jit(solution)/shard_map/ppermute | solution.py:216
  84.8 27.6 %collective-permute-start.13 = (bf16[4,24,2304]{2,1,0:T(8,128)(2,1)S(1)}, bf16[4,24,2304]{2,1,0:T(8,128)(2,1)}, u32[]{:S(2)}, u32[]{:S(2)}) collective-permute-start(bf16[4,24,2304]{2,1,0:T(8,128)(2,1)S(1)} %pad_maximum_fusion.9.refs_0_), channel_id=1, source_target_pairs={{0,1},{1,0},{2,3},{3,2},{4,5},{5,4},{6,7},{7,6},{8,9},{9,8},{10,11... | collective-permute-start | bytes 1327112 | tf_op jit(solution)/shard_map/ppermute | solution.py:216
  87.4 26.7 %collective-permute-start.15 = (bf16[4,24,2304]{2,1,0:T(8,128)(2,1)}, bf16[4,24,2304]{2,1,0:T(8,128)(2,1)}, u32[]{:S(2)}, u32[]{:S(2)}) collective-permute-start(bf16[4,24,2304]{2,1,0:T(8,128)(2,1)} %collective-permute-done.14.refs_2_), channel_id=1, source_target_pairs={{0,1},{1,0},{2,3},{3,2},{4,5},{5,4},{6,7},{7,6},{8,9},{9,8},{10,11... | collective-permute-start | bytes 1327112 | tf_op jit(solution)/shard_map/ppermute | solution.py:216
  89.3 25.5 %collective-permute-start.17 = (bf16[4,24,2304]{2,1,0:T(8,128)(2,1)}, bf16[4,24,2304]{2,1,0:T(8,128)(2,1)}, u32[]{:S(2)}, u32[]{:S(2)}) collective-permute-start(bf16[4,24,2304]{2,1,0:T(8,128)(2,1)} %collective-permute-done.16.refs_4_), channel_id=1, source_target_pairs={{0,1},{1,0},{2,3},{3,2},{4,5},{5,4},{6,7},{7,6},{8,9},{9,8},{10,11... | collective-permute-start | bytes 1327112 | tf_op jit(solution)/shard_map/ppermute | solution.py:216
  98.8 17.5 %collective-permute-start.19 = (bf16[4,24,2304]{2,1,0:T(8,128)(2,1)}, bf16[4,24,2304]{2,1,0:T(8,128)(2,1)}, u32[]{:S(2)}, u32[]{:S(2)}) collective-permute-start(bf16[4,24,2304]{2,1,0:T(8,128)(2,1)} %collective-permute-done.18.refs_6_), channel_id=1, source_target_pairs={{0,1},{1,0},{2,3},{3,2},{4,5},{5,4},{6,7},{7,6},{8,9},{9,8},{10,11... | collective-permute-start | bytes 1327112 | tf_op jit(solution)/shard_map/ppermute | solution.py:216
  112.4 74.6 %collective-permute-start.34 = (bf16[4,24,3072]{2,1,0:T(8,128)(2,1)S(1)}, bf16[4,24,3072]{2,1,0:T(8,128)(2,1)}, u32[]{:S(2)}, u32[]{:S(2)}) collective-permute-start(bf16[4,24,3072]{2,1,0:T(8,128)(2,1)S(1)} %pad_maximum_fusion.7.refs_0_), channel_id=1, source_target_pairs={{0,2},{1,3},{2,0},{3,1},{4,6},{5,7},{6,4},{7,5},{8,10},{9,11},{10,... | collective-permute-start | bytes 1769480 | tf_op jit(solution)/shard_map/ppermute | solution.py:216
  113.9 73.1 %collective-permute-start.33 = (bf16[4,24,3072]{2,1,0:T(8,128)(2,1)S(1)}, bf16[4,24,3072]{2,1,0:T(8,128)(2,1)}, u32[]{:S(2)}, u32[]{:S(2)}) collective-permute-start(bf16[4,24,3072]{2,1,0:T(8,128)(2,1)S(1)} %pad_maximum_fusion.7.refs_0_), channel_id=1, source_target_pairs={{0,1},{1,0},{2,3},{3,2},{4,5},{5,4},{6,7},{7,6},{8,9},{9,8},{10,11... | collective-permute-start | bytes 1769480 | tf_op jit(solution)/shard_map/ppermute | solution.py:216
  114.2 73.4 %collective-permute-start.44 = (bf16[4,96,768]{2,1,0:T(8,128)(2,1)S(1)}, bf16[4,96,768]{2,1,0:T(8,128)(2,1)}, u32[]{:S(2)}, u32[]{:S(2)}) collective-permute-start(bf16[4,96,768]{2,1,0:T(8,128)(2,1)S(1)} %pad_maximum_fusion.8.refs_0_), channel_id=1, source_target_pairs={{0,2},{1,3},{2,0},{3,1},{4,6},{5,7},{6,4},{7,5},{8,10},{9,11},{10,... | collective-permute-start | bytes 1769480 | tf_op jit(solution)/shard_map/ppermute | solution.py:216
  114.7 74.0 %collective-permute-start.46 = (bf16[4,96,768]{2,1,0:T(8,128)(2,1)S(1)}, bf16[4,96,768]{2,1,0:T(8,128)(2,1)}, u32[]{:S(2)}, u32[]{:S(2)}) collective-permute-start(bf16[4,96,768]{2,1,0:T(8,128)(2,1)S(1)} %pad_maximum_fusion.8.refs_0_), channel_id=1, source_target_pairs={{0,4},{1,5},{2,6},{3,7},{4,0},{5,1},{6,2},{7,3},{8,12},{9,13},{10,... | collective-permute-start | bytes 1769480 | tf_op jit(solution)/shard_map/ppermute | solution.py:216
  116.2 72.1 %collective-permute-start.38 = (bf16[4,24,3072]{2,1,0:T(8,128)(2,1)S(1)}, bf16[4,24,3072]{2,1,0:T(8,128)(2,1)}, u32[]{:S(2)}, u32[]{:S(2)}) collective-permute-start(bf16[4,24,3072]{2,1,0:T(8,128)(2,1)S(1)} %collective-permute-done.36.refs_4_), channel_id=1, source_target_pairs={{0,2},{1,3},{2,0},{3,1},{4,6},{5,7},{6,4},{7,5},{8,10},{9,11},{10,... | collective-permute-start | bytes 1769480 | tf_op jit(solution)/shard_map/ppermute | solution.py:216
  187.6 15.5 %collective-permute-start.48 = (bf16[4,96,768]{2,1,0:T(8,128)(2,1)}, bf16[4,96,768]{2,1,0:T(8,128)(2,1)S(1)}, u32[]{:S(2)}, u32[]{:S(2)}) collective-permute-start(bf16[4,96,768]{2,1,0:T(8,128)(2,1)} %collective-permute-done.44.refs_2_), channel_id=1, source_target_pairs={{0,4},{1,5},{2,6},{3,7},{4,0},{5,1},{6,2},{7,3},{8,12},{9,13},{10,... | collective-permute-start | bytes 1769480 | tf_op jit(solution)/shard_map/ppermute | solution.py:216
  188.7 57.0 %collective-permute-start.43 = (bf16[4,96,768]{2,1,0:T(8,128)(2,1)S(1)}, bf16[4,96,768]{2,1,0:T(8,128)(2,1)S(1)}, u32[]{:S(2)}, u32[]{:S(2)}) collective-permute-start(bf16[4,96,768]{2,1,0:T(8,128)(2,1)S(1)} %pad_maximum_fusion.8.refs_0_), channel_id=1, source_target_pairs={{0,1},{1,0},{2,3},{3,2},{4,5},{5,4},{6,7},{7,6},{8,9},{9,8},{10,11... | collective-permute-start | bytes 1769480 | tf_op jit(solution)/shard_map/ppermute | solution.py:216
  189.3 56.5 %collective-permute-start.45 = (bf16[4,96,768]{2,1,0:T(8,128)(2,1)}, bf16[4,96,768]{2,1,0:T(8,128)(2,1)S(1)}, u32[]{:S(2)}, u32[]{:S(2)}) collective-permute-start(bf16[4,96,768]{2,1,0:T(8,128)(2,1)} %collective-permute-done.44.refs_2_), channel_id=1, source_target_pairs={{0,1},{1,0},{2,3},{3,2},{4,5},{5,4},{6,7},{7,6},{8,9},{9,8},{10,11... | collective-permute-start | bytes 1769480 | tf_op jit(solution)/shard_map/ppermute | solution.py:216
  190.1 55.7 %collective-permute-start.47 = (bf16[4,96,768]{2,1,0:T(8,128)(2,1)}, bf16[4,96,768]{2,1,0:T(8,128)(2,1)S(1)}, u32[]{:S(2)}, u32[]{:S(2)}) collective-permute-start(bf16[4,96,768]{2,1,0:T(8,128)(2,1)} %collective-permute-done.46.refs_4_), channel_id=1, source_target_pairs={{0,1},{1,0},{2,3},{3,2},{4,5},{5,4},{6,7},{7,6},{8,9},{9,8},{10,11... | collective-permute-start | bytes 1769480 | tf_op jit(solution)/shard_map/ppermute | solution.py:216
  203.1 42.7 %collective-permute-start.49 = (bf16[4,96,768]{2,1,0:T(8,128)(2,1)S(1)}, bf16[4,96,768]{2,1,0:T(8,128)(2,1)S(1)}, u32[]{:S(2)}, u32[]{:S(2)}) collective-permute-start(bf16[4,96,768]{2,1,0:T(8,128)(2,1)S(1)} %collective-permute-done.48.refs_6_), channel_id=1, source_target_pairs={{0,1},{1,0},{2,3},{3,2},{4,5},{5,4},{6,7},{7,6},{8,9},{9,8},{10,11... | collective-permute-start | bytes 1769480 | tf_op jit(solution)/shard_map/ppermute | solution.py:216
  442.0 72.7 %collective-permute-start.78 = (bf16[4,2,2,96,768]{4,3,0,2,1:T(8,128)(2,1)}, bf16[4,2,2,96,768]{4,3,0,2,1:T(8,128)(2,1)}, u32[]{:S(2)}, u32[]{:S(2)}) collective-permute-start(bf16[4,2,2,96,768]{4,3,0,2,1:T(8,128)(2,1)} %bitcast.328), channel_id=1, source_target_pairs={{0,1},{1,0},{2,3},{3,2},{4,5},{5,4},{6,7},{7,6},{8,9},{9,8},{10,11... | collective-permute-start | bytes 7077896 | tf_op jit(solution)/shard_map/ppermute | solution.py:216
  451.9 79.2 %collective-permute-start.72 = (bf16[4,2,2,24,3072]{4,3,0,1,2:T(8,128)(2,1)}, bf16[4,2,2,24,3072]{4,3,0,1,2:T(8,128)(2,1)}, u32[]{:S(2)}, u32[]{:S(2)}) collective-permute-start(bf16[4,2,2,24,3072]{4,3,0,1,2:T(8,128)(2,1)} %bitcast.329), channel_id=1, source_target_pairs={{0,1},{1,0},{2,3},{3,2},{4,5},{5,4},{6,7},{7,6},{8,9},{9,8},{10,11... | collective-permute-start | bytes 7077896 | tf_op jit(solution)/shard_map/ppermute | solution.py:216
  456.8 32.0 %collective-permute-start.66 = (bf16[4,2,2,24,768]{4,3,0,2,1:T(8,128)(2,1)}, bf16[4,2,2,24,768]{4,3,0,2,1:T(8,128)(2,1)}, u32[]{:S(2)}, u32[]{:S(2)}) collective-permute-start(bf16[4,2,2,24,768]{4,3,0,2,1:T(8,128)(2,1)} %bitcast.331), channel_id=1, source_target_pairs={{0,1},{1,0},{2,3},{3,2},{4,5},{5,4},{6,7},{7,6},{8,9},{9,8},{10,11... | collective-permute-start | bytes 1769480 | tf_op jit(solution)/shard_map/ppermute | solution.py:216
  487.9 20.0 %collective-permute-start.55 = (bf16[4,2,2,24,2304]{4,3,0,1,2:T(8,128)(2,1)S(1)}, bf16[4,2,2,24,2304]{4,3,0,1,2:T(8,128)(2,1)S(1)}, u32[]{:S(2)}, u32[]{:S(2)}) collective-permute-start(bf16[4,2,2,24,2304]{4,3,0,1,2:T(8,128)(2,1)S(1)} %bitcast.390), channel_id=1, source_target_pairs={{0,1},{1,0},{2,3},{3,2},{4,5},{5,4},{6,7},{7,6},{8,9},{9,8},{10,11... | collective-permute-start | bytes 5308424 | tf_op jit(solution)/shard_map/ppermute | solution.py:216
  512.1 17.7 %collective-permute-start.56 = (bf16[4,2,24,2304]{3,2,0,1:T(8,128)(2,1)S(1)}, bf16[4,2,24,2304]{3,2,0,1:T(8,128)(2,1)S(1)}, u32[]{:S(2)}, u32[]{:S(2)}) collective-permute-start(bf16[4,2,24,2304]{3,2,0,1:T(8,128)(2,1)S(1)} %dynamic-slice_bitcast_fusion.2), channel_id=1, source_target_pairs={{0,2},{1,3},{2,0},{3,1},{4,6},{5,7},{6,4},{7,5},{8,10},{9,11},{10,... | collective-permute-start | bytes 2654216 | tf_op jit(solution)/shard_map/ppermute | solution.py:216
  517.2 37.5 %collective-permute-start.79 = (bf16[4,2,96,768]{3,2,0,1:T(8,128)(2,1)S(1)}, bf16[4,2,96,768]{3,2,0,1:T(8,128)(2,1)S(1)}, u32[]{:S(2)}, u32[]{:S(2)}) collective-permute-start(bf16[4,2,96,768]{3,2,0,1:T(8,128)(2,1)S(1)} %dynamic-slice_bitcast_fusion), channel_id=1, source_target_pairs={{0,4},{1,5},{2,6},{3,7},{4,0},{5,1},{6,2},{7,3},{8,12},{9,13},{10,... | collective-permute-start | bytes 3538952 | tf_op jit(solution)/shard_map/ppermute | solution.py:216
  530.1 20.4 %collective-permute-start.57 = (bf16[4,24,2304]{2,1,0:T(8,128)(2,1)S(1)}, bf16[4,24,2304]{2,1,0:T(8,128)(2,1)S(1)}, u32[]{:S(2)}, u32[]{:S(2)}) collective-permute-start(bf16[4,24,2304]{2,1,0:T(8,128)(2,1)S(1)} %dynamic-slice_bitcast_fusion.5), channel_id=1, source_target_pairs={{0,4},{1,5},{2,6},{3,7},{4,0},{5,1},{6,2},{7,3},{8,12},{9,13},{10,... | collective-permute-start | bytes 1327112 | tf_op jit(solution)/shard_map/ppermute | solution.py:216
  533.7 27.6 %collective-permute-start.73 = (bf16[4,2,24,3072]{3,2,0,1:T(8,128)(2,1)S(1)}, bf16[4,2,24,3072]{3,2,0,1:T(8,128)(2,1)S(1)}, u32[]{:S(2)}, u32[]{:S(2)}) collective-permute-start(bf16[4,2,24,3072]{3,2,0,1:T(8,128)(2,1)S(1)} %dynamic-slice_bitcast_fusion.1), channel_id=1, source_target_pairs={{0,2},{1,3},{2,0},{3,1},{4,6},{5,7},{6,4},{7,5},{8,10},{9,11},{10,... | collective-permute-start | bytes 3538952 | tf_op jit(solution)/shard_map/ppermute | solution.py:216
  574.3 18.6 %collective-permute-start.76 = (bf16[24,3072]{1,0:T(8,128)(2,1)S(1)}, bf16[24,3072]{1,0:T(8,128)(2,1)S(1)}, u32[]{:S(2)}, u32[]{:S(2)}) collective-permute-start(bf16[24,3072]{1,0:T(8,128)(2,1)S(1)} %get-tuple-element.145), channel_id=1, source_target_pairs={{0,16},{1,17},{2,18},{3,19},{4,20},{5,21},{6,22},{7,23},{8,24},{9,... | collective-permute-start | bytes 442376 | tf_op jit(solution)/shard_map/ppermute | solution.py:216
  (207 other events, 1755.6 us)

commit v2 on v0

v2 whole, which is shorter than its diff:
```python
import functools
import math

import jax
import jax.numpy as jnp
from jax import lax
from jax.experimental import pallas as pl
from jax.experimental.pallas import tpu as pltpu
from jax.sharding import PartitionSpec as P

HD = 64
EPSILON = 1e-05
NEGATIVE = -1e30
TILE = 256
CHUNK = 512
NT = (((1,), (1,)), ((), ()))
TN = (((0,), (0,)), ((), ()))
NN = (((1,), (0,)), ((), ()))
ANY = pl.BlockSpec(memory_space=pl.ANY)
SCALARS = pl.BlockSpec(memory_space=pltpu.SMEM)
GRANT = pltpu.CompilerParams(vmem_limit_bytes=58 << 20)


def dot(left, right, dims=NN):
    return lax.dot_general(left, right, dims, preferred_element_type=jnp.float32)


def wide(values):
    return values.astype(jnp.float32)


def low(values):
    return values.astype(jnp.bfloat16)


def cost(flops, size):
    return pl.CostEstimate(flops=int(0.4 * flops), transcendentals=0, bytes_accessed=int(0.4 * size))


def standardize(values):
    center = values - jnp.mean(values, axis=1, keepdims=True)
    scale = lax.rsqrt(jnp.mean(center * center, axis=1, keepdims=True) + EPSILON)
    return center * scale, scale


def standardize_back(grads, normal, scale, gain):
    inner = grads * gain
    return (
        inner
        - jnp.mean(inner, axis=1, keepdims=True)
        - normal * jnp.mean(inner * normal, axis=1, keepdims=True)
    ) * scale


def fold_rows(values):
    return jnp.sum(values.reshape(-1, 8, values.shape[1]), axis=0)


def fetch(spots_ref, sources, target, sem, start=0):
    stop = start + target.shape[1]
    if len(sources) == 1:
        return [pltpu.make_async_copy(sources[0].at[:, pl.ds(start, stop - start)], target, sem.at[0])]
    rows = sources[0].shape[1]
    left = sources[6].shape[2] if len(sources) > 8 else 0
    copies = []
    for part, source in enumerate(sources):
        begin = left if part >= 8 else 0
        low_end, high_end = max(start, begin), min(stop, begin + source.shape[2])
        if low_end >= high_end:
            continue
        for step in range(4):
            spot = pl.multiple_of(spots_ref[(part - 2 if part >= 8 else part) * 4 + step] * rows, math.gcd(rows, 128))
            copies.append(
                pltpu.make_async_copy(
                    source.at[step, :, pl.ds(low_end - begin, high_end - low_end)],
                    target.at[pl.ds(spot, rows), pl.ds(low_end - start, high_end - low_end)],
                    sem.at[len(copies)],
                )
            )
    return copies


def run_all(copies):
    for copy in copies:
        copy.start()
    for copy in copies:
        copy.wait()


def first():
    return pl.program_id(0) == 0


def rows_of(columns):
    return pl.BlockSpec((TILE, columns), lambda block: (block, 0))


def whole(shape):
    return pl.BlockSpec(shape, lambda block: (0,) * len(shape))


def project_kernel(count, spots_ref, x_ref, vectors_ref, bias_ref, *refs):
    sources, (hidden_ref, out_ref, weight_ref, sem) = refs[:count], refs[count:]

    @pl.when(first())
    def _():
        run_all(fetch(spots_ref, sources, weight_ref, sem))

    normal, _ = standardize(wide(x_ref[...]))
    hidden = low(normal * vectors_ref[6:7, :] + vectors_ref[7:8, :])
    hidden_ref[...] = hidden
    width = hidden.shape[1]
    for part in range(3):
        columns = slice(part * width, (part + 1) * width)
        out_ref[:, columns] = low(dot(hidden, weight_ref[:, columns]) + bias_ref[:, columns])


def project(spots, tokens, vectors, bias, weight):
    slots, width = tokens.shape
    return pl.pallas_call(
        functools.partial(project_kernel, len(weight)),
        grid=(slots // TILE,),
        out_shape=(
            jax.ShapeDtypeStruct((slots, width), jnp.bfloat16),
            jax.ShapeDtypeStruct((slots, 3 * width), jnp.bfloat16),
        ),
        in_specs=[SCALARS, rows_of(width), whole(vectors.shape), whole((1, 3 * width))]
        + [ANY] * len(weight),
        out_specs=(rows_of(width), rows_of(3 * width)),
        scratch_shapes=[pltpu.VMEM((width, 3 * width), jnp.bfloat16), pltpu.SemaphoreType.DMA((40,))],
        compiler_params=GRANT,
        cost_estimate=cost(6 * slots * width * width, 20 * slots * width),
        name="project",
    )(spots, tokens, vectors, bias, *weight)


def bell(values):
    square = jnp.exp(values * values * -0.5)
    step = 1.0 / (1.0 + jnp.abs(values) * (0.3275911 * math.sqrt(0.5)))
    series = step * (
        0.5 * 0.254829592
        + step
        * (
            0.5 * -0.284496736
            + step * (0.5 * 1.421413741 + step * (0.5 * -1.453152027 + step * (0.5 * 1.061405429)))
        )
    )
    tail = series * square
    below = jnp.where(values > 0, 1.0 - tail, tail)
    return values * below, below + values * square * (1.0 / math.sqrt(2.0 * math.pi))


def lift_kernel(count, spots_ref, attended_ref, x_ref, vectors_ref, up_bias_ref, gain_ref, shift_ref, *refs):
    sources = refs[:count]
    (two_ref, middle_ref, three_ref, four_ref, normal_ref, slope_ref, out_ref, up_ref, active, out_sem, up_sem) = refs[count:]

    @pl.when(first())
    def _():
        run_all(
            fetch(spots_ref, sources, out_ref, out_sem)
            + fetch(spots_ref, sources, up_ref, up_sem, out_ref.shape[1])
        )

    mid_gain, mid_bias, out_bias, ffn_gain, ffn_bias = [vectors_ref[row : row + 1, :] for row in range(5)]
    normal, _ = standardize(attended_ref[...])
    two = low(normal * mid_gain + mid_bias)
    two_ref[...] = two
    middle = wide(x_ref[...]) + dot(two, out_ref[...]) + out_bias
    middle_ref[...] = middle
    normal, _ = standardize(middle)
    three = low(normal * ffn_gain + ffn_bias)
    three_ref[...] = three
    units = up_ref.shape[1]
    spans = [slice(start, start + CHUNK) for start in range(0, units, CHUNK)]
    raise_up = lambda span: dot(three, up_ref[:, span]) + up_bias_ref[:, span]
    ahead = raise_up(spans[0])
    total = jnp.zeros((TILE, 1), jnp.float32)
    slopes = []
    for number, span in enumerate(spans):
        upward = ahead
        if number + 1 < len(spans):
            ahead = raise_up(spans[number + 1])
        value, slope = bell(upward)
        active[:, span] = value
        slope_ref[:, span] = low(slope)
        total = total + jnp.sum(value, axis=1, keepdims=True)
    mean = total * (1.0 / units)
    spread = jnp.zeros((TILE, 1), jnp.float32)
    for span in spans:
        center = active[:, span] - mean
        spread = spread + jnp.sum(center * center, axis=1, keepdims=True)
    scale = lax.rsqrt(spread * (1.0 / units) + EPSILON)
    for span in spans:
        normal = (active[:, span] - mean) * scale
        normal_ref[:, span] = low(normal)
        four_ref[:, span] = low(normal * gain_ref[:, span] + shift_ref[:, span])
        slope_ref[:, span] = low(wide(slope_ref[:, span]) * scale)


def lift(spots, attended, tokens, vectors, up_bias, gain, shift, weight):
    slots, width = tokens.shape
    units = up_bias.shape[1]
    shape = jax.ShapeDtypeStruct
    return pl.pallas_call(
        functools.partial(lift_kernel, len(weight)),
        grid=(slots // TILE,),
        out_shape=(
            shape((slots, width), jnp.bfloat16),
            shape((slots, width), jnp.float32),
            shape((slots, width), jnp.bfloat16),
            shape((slots, units), jnp.bfloat16),
            shape((slots, units), jnp.bfloat16),
            shape((slots, units), jnp.bfloat16),
        ),
        in_specs=[SCALARS, rows_of(width), rows_of(width), whole(vectors.shape)]
        + [whole((1, units))] * 3
        + [ANY] * len(weight),
        out_specs=(rows_of(width),) * 3 + (rows_of(units),) * 3,
        scratch_shapes=[
            pltpu.VMEM((width, width), jnp.bfloat16),
            pltpu.VMEM((width, units), jnp.bfloat16),
            pltpu.VMEM((TILE, units), jnp.float32),
            pltpu.SemaphoreType.DMA((40,)),
            pltpu.SemaphoreType.DMA((40,)),
        ],
        compiler_params=GRANT,
        cost_estimate=cost(2 * slots * width * (width + units), 40 * slots * width),
        name="lift",
    )(spots, attended, tokens, vectors, up_bias, gain, shift, *weight)


def drop_kernel(count, spots_ref, middle_ref, four_ref, normal_ref, slope_ref, grad_ref, gain_ref, bias_ref, *refs):
    sources = refs[:count]
    out_ref, up_ref, sums_ref, weight_ref, keep, gain_acc, shift_acc, up_acc, down_acc, sem = refs[count:]

    @pl.when(first())
    def _():
        run_all(fetch(spots_ref, sources, weight_ref, sem))
        for acc in (gain_acc, shift_acc, up_acc, down_acc):
            acc[...] = jnp.zeros_like(acc)

    units = four_ref.shape[1]
    width = middle_ref.shape[1]
    grads = grad_ref[...]
    spans = [slice(start, start + CHUNK) for start in range(0, units, CHUNK)]
    back = lambda span: dot(grads, weight_ref[span, :], NT)
    ahead = back(spans[0])
    total = jnp.zeros((TILE, 1), jnp.float32)
    cross = jnp.zeros((TILE, 1), jnp.float32)
    for number, span in enumerate(spans):
        hidden = ahead
        if number + 1 < len(spans):
            ahead = back(spans[number + 1])
        normal = wide(normal_ref[:, span])
        shift_acc[:, span] += fold_rows(hidden)
        gain_acc[:, span] += fold_rows(hidden * normal)
        inner = hidden * gain_ref[:, span]
        keep[:, span] = inner
        total = total + jnp.sum(inner, axis=1, keepdims=True)
        cross = cross + jnp.sum(inner * normal, axis=1, keepdims=True)
    out_ref[...] = low(middle_ref[...] + dot(four_ref[...], weight_ref[...]) + bias_ref[...])
    total = total * (1.0 / units)
    cross = cross * (1.0 / units)
    for span in spans:
        up = (keep[:, span] - total - wide(normal_ref[:, span]) * cross) * wide(slope_ref[:, span])
        up = low(up)
        up_ref[:, span] = up
        up_acc[:, span] += fold_rows(wide(up))
    down_acc[...] += fold_rows(wide(grads))

    @pl.when(pl.program_id(0) == pl.num_programs(0) - 1)
    def _():
        sums_ref[...] = jnp.zeros_like(sums_ref)
        row = 0
        for acc in (gain_acc, shift_acc, up_acc, down_acc):
            for start in range(0, acc.shape[1], width):
                sums_ref[row : row + 1, :] = jnp.sum(acc[:, start : start + width], axis=0, keepdims=True)
                row += 1


def drop(spots, middle, four, normal, slope, grads, gain, bias, weight):
    slots, width = middle.shape
    units = four.shape[1]
    rows = 3 * units // width + 1
    return pl.pallas_call(
        functools.partial(drop_kernel, len(weight)),
        grid=(slots // TILE,),
        out_shape=(
            jax.ShapeDtypeStruct((slots, width), jnp.bfloat16),
            jax.ShapeDtypeStruct((slots, units), jnp.bfloat16),
            jax.ShapeDtypeStruct((rows, width), jnp.float32),
        ),
        in_specs=[SCALARS, rows_of(width)]
        + [rows_of(units)] * 3
        + [rows_of(width), whole((1, units)), whole((1, width))]
        + [ANY] * len(weight),
        out_specs=(rows_of(width), rows_of(units), whole((rows, width))),
        scratch_shapes=[
            pltpu.VMEM((units, width), jnp.bfloat16),
            pltpu.VMEM((TILE, units), jnp.float32),
            pltpu.VMEM((8, units), jnp.float32),
            pltpu.VMEM((8, units), jnp.float32),
            pltpu.VMEM((8, units), jnp.float32),
            pltpu.VMEM((8, width), jnp.float32),
            pltpu.SemaphoreType.DMA((40,)),
        ],
        compiler_params=GRANT,
        cost_estimate=cost(4 * slots * width * units, 40 * slots * width),
        name="drop",
    )(spots, middle, four, normal, slope, grads, gain, bias, *weight)


def settle_kernel(count, spots_ref, up_ref, middle_ref, grad_ref, attended_ref, ffn_gain_ref, mid_gain_ref, *refs):
    sources = refs[:count]
    (total_ref, branch_ref, back_ref, sums_ref, up_weight, out_weight, acc, up_sem, out_sem) = refs[count:]

    @pl.when(first())
    def _():
        run_all(
            fetch(spots_ref, sources, out_weight, out_sem)
            + fetch(spots_ref, sources, up_weight, up_sem, out_weight.shape[1])
        )
        acc[...] = jnp.zeros_like(acc)

    three = dot(up_ref[...], up_weight[...], NT)
    normal, scale = standardize(middle_ref[...])
    acc[0] += fold_rows(three * normal)
    acc[1] += fold_rows(three)
    total = wide(grad_ref[...]) + standardize_back(three, normal, scale, ffn_gain_ref[...])
    total_ref[...] = total
    branch = low(total)
    branch_ref[...] = branch
    acc[2] += fold_rows(wide(branch))
    two = dot(branch, out_weight[...], NT)
    normal, scale = standardize(attended_ref[...])
    acc[3] += fold_rows(two * normal)
    acc[4] += fold_rows(two)
    back_ref[...] = low(standardize_back(two, normal, scale, mid_gain_ref[...]))

    @pl.when(pl.program_id(0) == pl.num_programs(0) - 1)
    def _():
        sums_ref[...] = jnp.zeros_like(sums_ref)
        for row in range(5):
            sums_ref[row : row + 1, :] = jnp.sum(acc[row], axis=0, keepdims=True)


def settle(spots, up, middle, grads, attended, ffn_gain, mid_gain, weight):
    slots, width = middle.shape
    units = up.shape[1]
    return pl.pallas_call(
        functools.partial(settle_kernel, len(weight)),
        grid=(slots // TILE,),
        out_shape=(
            jax.ShapeDtypeStruct((slots, width), jnp.float32),
            jax.ShapeDtypeStruct((slots, width), jnp.bfloat16),
            jax.ShapeDtypeStruct((slots, width), jnp.bfloat16),
            jax.ShapeDtypeStruct((8, width), jnp.float32),
        ),
        in_specs=[SCALARS, rows_of(units)]
        + [rows_of(width)] * 3
        + [whole((1, width))] * 2
        + [ANY] * len(weight),
        out_specs=(rows_of(width),) * 3 + (whole((8, width)),),
        scratch_shapes=[
            pltpu.VMEM((width, units), jnp.bfloat16),
            pltpu.VMEM((width, width), jnp.bfloat16),
            pltpu.VMEM((5, 8, width), jnp.float32),
            pltpu.SemaphoreType.DMA((40,)),
            pltpu.SemaphoreType.DMA((40,)),
        ],
        compiler_params=GRANT,
        cost_estimate=cost(2 * slots * width * (units + width), 30 * slots * width),
        name="settle",
    )(spots, up, middle, grads, attended, ffn_gain, mid_gain, *weight)


def finish_kernel(count, spots_ref, q_ref, k_ref, v_ref, x_ref, total_ref, gain_ref, *refs):
    sources, (out_ref, sums_ref, weight_ref, acc, sem) = refs[:count], refs[count:]

    @pl.when(first())
    def _():
        run_all(fetch(spots_ref, sources, weight_ref, sem))
        acc[...] = jnp.zeros_like(acc)

    width = x_ref.shape[1]
    one = dot(q_ref[...], weight_ref[:, :width], NT)
    one = one + dot(k_ref[...], weight_ref[:, width : 2 * width], NT)
    one = one + dot(v_ref[...], weight_ref[:, 2 * width :], NT)
    normal, scale = standardize(wide(x_ref[...]))
    acc[0] += fold_rows(one * normal)
    acc[1] += fold_rows(one)
    acc[2] += fold_rows(wide(q_ref[...]))
    acc[3] += fold_rows(wide(v_ref[...]))
    out_ref[...] = total_ref[...] + standardize_back(one, normal, scale, gain_ref[...])

    @pl.when(pl.program_id(0) == pl.num_programs(0) - 1)
    def _():
        sums_ref[...] = jnp.zeros_like(sums_ref)
        for row in range(4):
            sums_ref[row : row + 1, :] = jnp.sum(acc[row], axis=0, keepdims=True)


def finish(spots, grad_q, grad_k, grad_v, tokens, total, gain, weight):
    slots, width = tokens.shape
    return pl.pallas_call(
        functools.partial(finish_kernel, len(weight)),
        grid=(slots // TILE,),
        out_shape=(
            jax.ShapeDtypeStruct((slots, width), jnp.float32),
            jax.ShapeDtypeStruct((8, width), jnp.float32),
        ),
        in_specs=[SCALARS]
        + [rows_of(width)] * 5
        + [whole((1, width))]
        + [ANY] * len(weight),
        out_specs=(rows_of(width), whole((8, width))),
        scratch_shapes=[
            pltpu.VMEM((width, 3 * width), jnp.bfloat16),
            pltpu.VMEM((4, 8, width), jnp.float32),
            pltpu.SemaphoreType.DMA((40,)),
        ],
        compiler_params=GRANT,
        cost_estimate=cost(6 * slots * width * width, 24 * slots * width),
        name="finish",
    )(spots, grad_q, grad_k, grad_v, tokens, total, gain, *weight)


def outer_kernel(rows, core_ref, left_ref, right_ref, *out_refs):
    product = dot(left_ref[...], right_ref[...], TN)
    if rows is None:
        out_refs[0][...] = product.astype(out_refs[0].dtype)
        return
    near = core_ref[0] == 0
    for chip in range(product.shape[0] // (2 * rows)):
        one = low(product[chip * 2 * rows : chip * 2 * rows + rows, :])
        two = low(product[chip * 2 * rows + rows : (chip + 1) * 2 * rows, :])
        out_refs[0][chip] = jnp.where(near, one, two)
        out_refs[1][chip] = jnp.where(near, two, one)


def outer(core, left, right, rows, name, dtype=jnp.float32):
    slots, height = left.shape
    columns = right.shape[1]
    step = min(height, columns)
    tall = height > columns
    left_spec = pl.BlockSpec((slots, step), (lambda block: (0, block)) if tall else (lambda block: (0, 0)))
    right_spec = pl.BlockSpec((slots, step), (lambda block: (0, 0)) if tall else (lambda block: (0, block)))
    if rows is None:
        out_shape = (jax.ShapeDtypeStruct((height, columns), dtype),)
        out_specs = (pl.BlockSpec((step, step), (lambda block: (block, 0)) if tall else (lambda block: (0, block))),)
    else:
        out_shape = (jax.ShapeDtypeStruct((height // (2 * rows), rows, columns), jnp.bfloat16),) * 2
        out_specs = (
            pl.BlockSpec(
                (step // (2 * rows), rows, step),
                (lambda block: (block, 0, 0)) if tall else (lambda block: (0, 0, block)),
            ),
        ) * 2
    return pl.pallas_call(
        functools.partial(outer_kernel, rows),
        grid=(max(height, columns) // step,),
        out_shape=out_shape,
        in_specs=[SCALARS, left_spec, right_spec],
        out_specs=out_specs,
        compiler_params=GRANT,
        cost_estimate=cost(2 * slots * height * columns, 2 * slots * (height + columns) + 4 * height * columns),
        name=name,
    )(core, left, right)


def outer_three_kernel(rows, core_ref, left_ref, q_ref, k_ref, v_ref, *out_refs):
    width = q_ref.shape[1]
    for part, right_ref in enumerate((q_ref, k_ref, v_ref)):
        columns = slice(part * width, (part + 1) * width)
        product = dot(left_ref[...], right_ref[...], TN)
        if rows is None:
            out_refs[0][:, columns] = product
            continue
        near = core_ref[0] == 0
        for chip in range(product.shape[0] // (2 * rows)):
            first_rows = low(product[chip * 2 * rows : chip * 2 * rows + rows, :])
            second_rows = low(product[chip * 2 * rows + rows : (chip + 1) * 2 * rows, :])
            out_refs[0][chip, :, columns] = jnp.where(near, first_rows, second_rows)
            out_refs[1][chip, :, columns] = jnp.where(near, second_rows, first_rows)


def outer_three(core, left, grads, rows):
    slots, width = left.shape
    if rows is None:
        out_shape = (jax.ShapeDtypeStruct((width, 3 * width), jnp.float32),)
    else:
        out_shape = (jax.ShapeDtypeStruct((width // (2 * rows), rows, 3 * width), jnp.bfloat16),) * 2
    return pl.pallas_call(
        functools.partial(outer_three_kernel, rows),
        out_shape=out_shape,
        in_specs=[SCALARS] + [pl.BlockSpec(memory_space=pltpu.VMEM)] * 4,
        out_specs=(pl.BlockSpec(memory_space=pltpu.VMEM),) * len(out_shape),
        compiler_params=GRANT,
        cost_estimate=cost(6 * slots * width * width, 8 * slots * width + 12 * width * width),
        name="outer_three",
    )(core, left, *grads)


def halves(values):
    lane = lax.broadcasted_iota(jnp.int32, values.shape, 1)
    zero = jnp.zeros_like(values)
    return jnp.where(lane < HD, values, zero), jnp.where(lane >= HD, values, zero)


def segment_starts(lengths_ref, position):
    start = jnp.zeros_like(position)
    end = jnp.int32(0)
    for index in range(lengths_ref.shape[1] - 1):
        end = end + lengths_ref[0, index]
        start = jnp.where(position >= end, end, start)
    return start


def fill_bias(tile, slots, lengths_ref, bias_ref):
    for block in range(slots // tile):
        reach = (block + 1) * tile
        spot = block * (block + 1) // 2 * tile
        query = lax.broadcasted_iota(jnp.int32, (reach, tile), 1) + block * tile
        key = lax.broadcasted_iota(jnp.int32, (reach, tile), 0)
        start = segment_starts(lengths_ref, lax.broadcasted_iota(jnp.int32, (1, tile), 1) + block * tile)
        bias_ref[spot : spot + reach, :] = jnp.where((key <= query) & (key >= start), 0.0, NEGATIVE)


def attend_kernel(tile, lengths_ref, q_ref, k_ref, v_ref, out_ref, total_ref, bias_ref):
    slots = q_ref.shape[0]

    @pl.when(pl.program_id(0) == 0)
    def _():
        fill_bias(tile, slots, lengths_ref, bias_ref)

    values = halves(v_ref[...])
    steps = [(block, head) for block in range(slots // tile) for head in range(2)]

    def score(block, head):
        reach = (block + 1) * tile
        spot = block * (block + 1) // 2 * tile
        query = halves(q_ref[block * tile : reach, :] * jnp.bfloat16(1.0 / math.sqrt(HD)))[head]
        return dot(k_ref[:reach, :], query, NT) + bias_ref[spot : spot + reach, :]

    ahead = score(*steps[0])
    for number, (block, head) in enumerate(steps):
        reach = (block + 1) * tile
        rows = slice(block * tile, reach)
        scores = ahead
        if number + 1 < len(steps):
            ahead = score(*steps[number + 1])
        top = jnp.max(scores, axis=0, keepdims=True)
        fresh = jnp.exp(scores - top)
        mass = jnp.sum(fresh, axis=0, keepdims=True)
        part = dot(values[head][:reach, :], fresh.astype(jnp.bfloat16), TN) * (1.0 / mass)
        mixed = part if head == 0 else mixed + part
        total_ref[0, head : head + 1, rows] = top + jnp.log(mass)
        if head:
            out_ref[rows, :] = mixed.T


def attend_forward(lengths, projected, begin, pairs, tile=256):
    slots, every = projected.shape[0], projected.shape[1] // (6 * HD)
    blocks = slots // tile
    column = lambda offset: pl.BlockSpec((slots, 2 * HD), lambda pair: (0, offset + pair))
    return pl.pallas_call(
        functools.partial(attend_kernel, tile),
        grid=(pairs,),
        out_shape=(
            jax.ShapeDtypeStruct((slots, 2 * HD * pairs), jnp.float32),
            jax.ShapeDtypeStruct((pairs, 8, slots), jnp.float32),
        ),
        in_specs=[pl.BlockSpec(memory_space=pltpu.SMEM), *[column(begin + part * every) for part in range(3)]],
        out_specs=(column(0), pl.BlockSpec((1, 8, slots), lambda pair: (pair, 0, 0))),
        scratch_shapes=[pltpu.VMEM((tile * blocks * (blocks + 1) // 2, tile), jnp.float32)],
        compiler_params=GRANT,
        cost_estimate=cost(20 * 10**9, 8 * 10**6),
        name="attend_forward",
    )(lengths, projected, projected, projected)


def attend_back_kernel(tile, lengths_ref, q_ref, k_ref, v_ref, g_ref, out_ref, total_ref, gq_ref, gk_ref, gv_ref, bias_ref, gk_acc, gv_acc):
    slots = q_ref.shape[0]

    @pl.when(pl.program_id(0) == 0)
    def _():
        fill_bias(tile, slots, lengths_ref, bias_ref)

    weighed = (g_ref[...].astype(jnp.float32) * out_ref[...]).T
    deltas = [
        jnp.sum(weighed[:HD, :], axis=0, keepdims=True),
        jnp.sum(weighed[HD:, :], axis=0, keepdims=True),
    ]
    keys = halves(k_ref[...])
    steps = [(block, head) for block in reversed(range(slots // tile)) for head in range(2)]

    def begin(block, head):
        reach = (block + 1) * tile
        spot = block * (block + 1) // 2 * tile
        rows = slice(block * tile, reach)
        query = halves(q_ref[rows, :] * jnp.bfloat16(1.0 / math.sqrt(HD)))[head]
        grad = halves(g_ref[rows, :])[head]
        scores = dot(k_ref[:reach, :], query, NT) + bias_ref[spot : spot + reach, :]
        return query, grad, scores, dot(v_ref[:reach, :], grad, NT)

    ahead = begin(*steps[0])
    for number, (block, head) in enumerate(steps):
        reach = (block + 1) * tile
        rows = slice(block * tile, reach)
        query, grad, scores, grad_soft = ahead
        if number + 1 < len(steps):
            ahead = begin(*steps[number + 1])
        soft = jnp.exp(scores - total_ref[0, head : head + 1, rows])
        grad_scores = (soft * (grad_soft - deltas[head][:, rows])).astype(jnp.bfloat16)
        gv = dot(soft.astype(jnp.bfloat16), grad)
        gk = dot(grad_scores, query)
        if number == 0:
            gk_acc[...] = gk
            gv_acc[...] = gv
        else:
            gk_acc[:reach, :] += gk
            gv_acc[:reach, :] += gv
        part = dot(keys[head][:reach, :], grad_scores, TN)
        gq = part if head == 0 else gq + part
        if head:
            gq_ref[rows, :] = (gq.T * (1.0 / math.sqrt(HD))).astype(jnp.bfloat16)
    gk_ref[...] = gk_acc[...].astype(jnp.bfloat16)
    gv_ref[...] = gv_acc[...].astype(jnp.bfloat16)


def attend_backward(lengths, projected, grad_out, attended, totals, begin, tile=256):
    slots, width = attended.shape
    pairs, every = width // (2 * HD), projected.shape[1] // (6 * HD)
    blocks = slots // tile
    column = lambda offset: pl.BlockSpec((slots, 2 * HD), lambda pair: (0, offset + pair))
    return pl.pallas_call(
        functools.partial(attend_back_kernel, tile),
        grid=(pairs,),
        out_shape=(jax.ShapeDtypeStruct((slots, width), jnp.bfloat16),) * 3,
        in_specs=[
            pl.BlockSpec(memory_space=pltpu.SMEM),
            *[column(begin + part * every) for part in range(3)],
            column(begin),
            column(0),
            pl.BlockSpec((1, 8, slots), lambda pair: (pair, 0, 0)),
        ],
        out_specs=(column(0),) * 3,
        scratch_shapes=[
            pltpu.VMEM((tile * blocks * (blocks + 1) // 2, tile), jnp.float32),
            pltpu.VMEM((slots, 2 * HD), jnp.float32),
            pltpu.VMEM((slots, 2 * HD), jnp.float32),
        ],
        compiler_params=GRANT,
        cost_estimate=cost(28 * 10**9, 12 * 10**6),
        name="attend_backward",
    )(lengths, projected, projected, projected, grad_out, attended, totals)


AXES = ("dp", "fsdp")


def place():
    outer_index, inner_index = lax.axis_index("dp"), lax.axis_index("fsdp")
    return outer_index // 2, outer_index % 2, inner_index // 2, inner_index % 2


def send(values, dz=0, dx=0, dy=0, dc=0):
    pairs = []
    for z in range(4):
        for x in range(2):
            for y in range(2):
                for c in range(2):
                    here = ((z * 2 + x) * 2 + y) * 2 + c
                    there = ((((z + dz) % 4) * 2 + (x ^ dx)) * 2 + (y ^ dy)) * 2 + (c ^ dc)
                    pairs.append((here, there))
    return lax.ppermute(values, AXES, pairs)


def index_of(z, x, y, c):
    return ((z * 2 + x) * 2 + y) * 2 + c


COLUMNS_Z = [[index_of(z, x, y, c) for z in range(4)] for x in range(2) for y in range(2) for c in range(2)]


def part_spots():
    z, x, y, c = place()
    spots = []
    for part in range(8):
        dx, dy, dc = part >> 2 & 1, part >> 1 & 1, part & 1
        for step in range(4):
            spots.append(((((z - step) % 4) * 2 + (x ^ dx)) * 2 + (y ^ dy)) * 2 + (c ^ dc))
    return jnp.stack(spots).astype(jnp.int32)


def after(value, *others):
    return lax.optimization_barrier((value, *others))[0]


def send_z(shard):
    return [shard] + [send(shard, dz=step) for step in (1, 2, 3)]


def gather_z(shards, *gate):
    return jnp.stack(after(shards, *gate))


def gather_near(own):
    return own, send(own, dy=1), send(own, dx=1), send(own, dx=1, dy=1)


def gather_core(parts):
    both = []
    for part in parts:
        both += [part, send(part, dc=1)]
    return both


def chips_kernel(way, place_ref, *refs):
    x, y = place_ref[1], place_ref[2]
    count = 4 if way == "both" else 2
    sources, out_refs = refs[:-count], refs[-count:]
    start = 0
    for kept_ref, got_ref in zip(sources[::2], sources[1::2]):
        columns = slice(start, start + kept_ref.shape[2])
        start = columns.stop
        total = lambda z, x, y: low(wide(kept_ref[(z * 2 + x) * 2 + y]) + wide(got_ref[(z * 2 + x) * 2 + y]))
        for z in range(4):
            for flip, out_ref in enumerate(out_refs):
                if way == "x":
                    for other in range(2):
                        out_ref[z * 2 + other, :, columns] = total(z, x ^ flip, other)
                elif way == "y":
                    for other in range(2):
                        out_ref[z * 2 + other, :, columns] = total(z, other, y ^ flip)
                else:
                    out_ref[z, :, columns] = total(z, x ^ (flip >> 1), y ^ (flip & 1))


def lines_kernel(axis, place_ref, kept_ref, got_ref, stay_ref, go_ref):
    for z in range(4):
        for flip, out_ref in enumerate((stay_ref, go_ref)):
            spot = z * 2 + (place_ref[axis] ^ flip)
            out_ref[z] = low(wide(kept_ref[spot]) + wide(got_ref[spot]))


def planes_kernel(count, place_ref, *refs):
    sources, mine_ref, out_refs = refs[:count], refs[count], refs[count + 1 :]
    for step in range(4):
        z = (place_ref[0] + step) & 3
        total = wide(sources[0][z])
        for source in sources[1:]:
            total = total + wide(source[z])
        if step == 0:
            mine_ref[...] = total
        else:
            out_refs[step - 1][...] = low(total)


def plane_kernel(count, place_ref, *refs):
    sources, out_ref = refs[:count], refs[count]
    for z in range(4):
        total = wide(sources[0][z])
        for source in sources[1:]:
            total = total + wide(source[z])
        out_ref[z] = low(total)


def small_call(kernel, spot, arrays, out_shapes, name):
    vmem = pl.BlockSpec(memory_space=pltpu.VMEM)
    moved = sum(math.prod(a.shape) * a.dtype.itemsize for a in (*arrays, *out_shapes))
    return pl.pallas_call(
        kernel,
        out_shape=tuple(out_shapes),
        in_specs=[SCALARS] + [vmem] * len(arrays),
        out_specs=(vmem,) * len(out_shapes),
        compiler_params=GRANT,
        cost_estimate=cost(0, moved),
        name=name,
    )(spot, *arrays)


class Sum:
    def __init__(self, spot, kept, given, way, name):
        self.spot, self.way, self.name = spot, way, name
        self.rows, self.columns = kept.shape[1], 0
        self.arrays = []
        self.add(kept, given)

    def add(self, kept, given):
        self.kept = kept
        self.columns += kept.shape[2]
        self.arrays += [kept, send(given, dc=1)]

    def shapes(self, blocks, count):
        return [jax.ShapeDtypeStruct((blocks, self.rows, self.columns), jnp.bfloat16)] * count

    def chips(self, *gate):
        kernel = functools.partial(chips_kernel, self.way)
        out = self.shapes(4, 4) if self.way == "both" else self.shapes(8, 2)
        out = small_call(kernel, self.spot, (after(self.arrays[0], *gate), *self.arrays[1:]), out, "chips_" + self.name)
        if self.way == "both":
            own, to_y, to_x, to_xy = out
            self.parts = [own, send(to_y, dy=1), send(to_x, dx=1), send(to_xy, dx=1, dy=1)]
        else:
            self.pair = out[0], send(out[1], dx=int(self.way == "x"), dy=int(self.way == "y"))
        return out[0]

    def lines(self, *gate):
        kernel = functools.partial(lines_kernel, 2 if self.way == "x" else 1)
        kept, got = self.pair
        own, go = small_call(kernel, self.spot, (after(kept, *gate), got), self.shapes(4, 2), "lines_" + self.name)
        self.parts = [own, send(go, dx=int(self.way == "y"), dy=int(self.way == "x"))]
        return own

    def planes(self, *gate):
        self.parts[0] = after(self.parts[0], *gate)
        shape = (self.rows, self.columns)
        out = [jax.ShapeDtypeStruct(shape, jnp.float32)] + [jax.ShapeDtypeStruct(shape, jnp.bfloat16)] * 3
        kernel = functools.partial(planes_kernel, len(self.parts))
        mine, *others = small_call(kernel, self.spot, self.parts, out, "planes_" + self.name)
        self.others = [send(other, dz=step + 1) for step, other in enumerate(others)]
        self.mine = mine
        return mine

    def done(self):
        return self.mine + sum(wide(other) for other in self.others)

    def plane(self, *gate):
        self.parts[0] = after(self.parts[0], *gate)
        kernel = functools.partial(plane_kernel, len(self.parts))
        (total,) = small_call(kernel, self.spot, self.parts, self.shapes(4, 1), "plane_" + self.name)
        flat = total.reshape(4 * self.rows, self.columns)
        mine = lax.psum_scatter(flat, AXES, scatter_dimension=0, axis_index_groups=COLUMNS_Z, tiled=True)
        return total, wide(mine)


WIDE = ("mid_gain", "mid_bias", "out_bias", "ffn_gain", "ffn_bias", "down_bias", "in_gain", "in_bias")
DEEP = ("up_bias", "hid_gain", "hid_bias")


def spread_row(packed, width, count):
    lane = lax.broadcasted_iota(jnp.int32, (1, count), 1)
    owner = jnp.zeros_like(lane)
    for device in range(1, 32):
        owner = owner + (lane >= device * width).astype(jnp.int32)
    inside = lane - owner * width
    pick = lax.broadcasted_iota(jnp.int32, (128, count), 0) == inside
    everyone = dot(packed, low(jnp.where(pick, 1.0, 0.0)))
    owned = lax.broadcasted_iota(jnp.int32, (32, count), 0) == owner
    return jnp.sum(jnp.where(owned, everyone, 0.0), axis=0, keepdims=True)


def vectors_kernel(spots_ref, *refs):
    sources, (wide_ref, qkv_ref, deep_ref, weight_ref, landed, everything, sem, weight_sem) = refs[:8], refs[8:]
    lanes = landed.shape[3]
    copies = [
        pltpu.make_async_copy(
            source.at[:, :, pl.ds(source.shape[2] - lanes, lanes)], landed.at[part], sem.at[part]
        )
        for part, source in enumerate(sources)
    ]
    laid = [
        pltpu.make_async_copy(
            source.at[step, :, pl.ds(0, weight_ref.shape[2])],
            weight_ref.at[spots_ref[part * 4 + step]],
            weight_sem.at[part * 4 + step],
        )
        for part, source in enumerate(sources)
        for step in range(4)
    ]
    for copy in laid:
        copy.start()
    run_all(copies)
    for part in range(8):
        for step in range(4):
            everything[spots_ref[part * 4 + step]] = wide(landed[part, step])
    row = lambda number: low(everything[:, number, :])
    width = wide_ref.shape[1]
    for number in range(8):
        wide_ref[number : number + 1, :] = spread_row(row(number), width // 32, width)
    both = spread_row(row(8), width // 16, 2 * width)
    qkv_ref[:, :width] = both[:, :width]
    qkv_ref[:, width : 2 * width] = jnp.zeros((1, width), jnp.float32)
    qkv_ref[:, 2 * width :] = both[:, width:]
    units = deep_ref.shape[2]
    for number in range(3):
        deep_ref[number] = spread_row(row(9 + number), units // 32, units)
    for copy in laid:
        copy.wait()


def pack_vectors(shards, rows):
    listed = [shards[name] for name in WIDE + ("qv_bias",) + DEEP]
    packed = jnp.stack([jnp.pad(entry, (0, 128 - entry.shape[0])) for entry in listed])
    return jnp.pad(packed, ((0, rows - packed.shape[0]), (0, 0)))


def unpack_first(spots, parts, width, units):
    vmem = pl.BlockSpec(memory_space=pltpu.VMEM)
    rows = parts[0].shape[1]
    *vectors, weight = pl.pallas_call(
        vectors_kernel,
        out_shape=(
            jax.ShapeDtypeStruct((8, width), jnp.float32),
            jax.ShapeDtypeStruct((1, 3 * width), jnp.float32),
            jax.ShapeDtypeStruct((3, 1, units), jnp.float32),
            jax.ShapeDtypeStruct((32, rows, 3 * width), jnp.bfloat16),
        ),
        in_specs=[SCALARS] + [ANY] * 8,
        out_specs=(vmem,) * 4,
        scratch_shapes=[
            pltpu.VMEM((8, 4, rows, 128), jnp.bfloat16),
            pltpu.VMEM((32, rows, 128), jnp.float32),
            pltpu.SemaphoreType.DMA((8,)),
            pltpu.SemaphoreType.DMA((32,)),
        ],
        compiler_params=GRANT,
        cost_estimate=cost(10**8, 10**7),
        name="unpack",
    )(spots, *parts)
    return vectors, weight.reshape(32 * rows, 3 * width)


def sum_rows_core(rows):
    return rows + send(rows, dc=1)


def sum_rows_near(rows):
    return rows + send(rows, dy=1) + (send(rows, dx=1) + send(rows, dx=1, dy=1))


def sum_rows_z(rows):
    return rows + send(rows, dz=1) + (send(rows, dz=2) + send(rows, dz=3))


def owners_kernel(core_ref, deep_ref, mid_ref, end_ref, *out_refs):
    near = core_ref[0] == 0
    width = mid_ref.shape[1]
    per = (deep_ref.shape[0] - 1) // 3
    row = lambda ref, number: ref[number : number + 1, :]
    narrow = [row(deep_ref, 3 * per)] + [row(mid_ref, number) for number in range(5)] + [row(end_ref, number) for number in range(2)]
    broad = [
        jnp.concatenate([row(deep_ref, number * per + part) for part in range(per)], axis=1) for number in range(3)
    ]
    pair = [jnp.concatenate([row(end_ref, 2), row(end_ref, 3)], axis=1)]
    start = 0
    for group in (narrow, broad, pair):
        group = group + [jnp.zeros_like(group[0])] * (8 - len(group))
        stacked = jnp.concatenate(group, axis=0)
        share = stacked.shape[1] // 32
        stacked = jnp.concatenate([stacked, jnp.zeros((8, 128), jnp.float32)], axis=1)
        blocks = [stacked[:, owner * share : owner * share + 128] for owner in range(32)]
        for chip in range(16):
            one, two = blocks[2 * chip], blocks[2 * chip + 1]
            out_refs[0][chip, start : start + 8, :] = jnp.where(near, one, two)
            out_refs[1][chip, start : start + 8, :] = jnp.where(near, two, one)
        start += 8


SUMMED = {
    "down_bias": 0,
    "ffn_gain": 1,
    "ffn_bias": 2,
    "out_bias": 3,
    "mid_gain": 4,
    "mid_bias": 5,
    "in_gain": 6,
    "in_bias": 7,
    "hid_gain": 8,
    "hid_bias": 9,
    "up_bias": 10,
    "qv_bias": 16,
}


def lay_vectors(core, deep, mid, end):
    vmem = pl.BlockSpec(memory_space=pltpu.VMEM)
    return pl.pallas_call(
        owners_kernel,
        out_shape=(jax.ShapeDtypeStruct((16, 24, 128), jnp.float32),) * 2,
        in_specs=[SCALARS] + [vmem] * 3,
        out_specs=(vmem,) * 2,
        compiler_params=GRANT,
        cost_estimate=cost(0, 10**6),
        name="owners",
    )(core, deep, mid, end)


def halve(values, axis, place_index):
    pick = functools.partial(lax.dynamic_index_in_dim, values, axis=axis, keepdims=False)
    return pick(place_index), pick(1 - place_index)


def sum_vectors(kept, got):
    z, x, y, _ = place()
    stay, go = halve((kept + got).reshape(4, 2, 2, *kept.shape[1:]), 1, x)
    stay, go = halve(stay + send(go, dx=1), 1, y)
    plane = stay + send(go, dy=1)
    turns = [lax.dynamic_index_in_dim(plane, (z + step) % 4, keepdims=False) for step in range(4)]
    return turns[0] + sum(send(turns[step], dz=step) for step in (1, 2, 3))


WEIGHTS = ("qkv_weight", "out_weight", "up_weight", "down_weight")
PARAMS = (
    "in_gain",
    "in_bias",
    "qkv_weight",
    "qv_bias",
    "mid_gain",
    "mid_bias",
    "out_weight",
    "out_bias",
    "ffn_gain",
    "ffn_bias",
    "up_weight",
    "up_bias",
    "hid_gain",
    "hid_bias",
    "down_weight",
    "down_bias",
)


def forward_staged(spots, tokens, lengths, shards):
    width = tokens.shape[1]
    units = 32 * shards["up_bias"].shape[0]
    rows = shards["qkv_weight"].shape[0]
    whole_piece = lambda shard: [lax.all_gather(shard, AXES, axis=0, tiled=True)]
    second_piece = whole_piece(jnp.concatenate([shards["out_weight"], shards["up_weight"]], axis=1))
    first_piece = jnp.concatenate([shards["qkv_weight"], pack_vectors(shards, rows)], axis=1)
    near_first = gather_near(gather_z(send_z(first_piece)))
    vectors, weight = unpack_first(spots, gather_core(near_first), width, units)
    third_piece = send_z(after(shards["down_weight"], near_first))
    return ([weight], second_piece, third_piece), vectors


def forward_plain(spots, tokens, lengths, shards):
    width = tokens.shape[1]
    full = {name: lax.all_gather(shards[name], AXES, axis=0, tiled=True) for name in PARAMS}
    pieces = (
        [full["qkv_weight"]],
        [jnp.concatenate([full["out_weight"], full["up_weight"]], axis=1)],
        [full["down_weight"]],
    )
    full = {name: wide(full[name]) for name in PARAMS if name not in WEIGHTS}
    rows = jnp.stack([full[name] for name in WIDE])
    bias = full["qv_bias"]
    qkv_bias = jnp.concatenate([bias[:width], jnp.zeros((width,), jnp.float32), bias[width:]])[None]
    return pieces, (rows, qkv_bias, jnp.stack([full[name][None] for name in DEEP]))


def body(staged, tokens, lengths, cotangent, *params):
    shards = dict(zip(PARAMS, params))
    width = tokens.shape[1]
    pairs = width // (2 * HD)
    if staged:
        spot = jnp.stack(place()).astype(jnp.int32)
        core, spots = spot[3:4], part_spots()
    else:
        spots = core = jnp.zeros((1,), jnp.int32)
    run = forward_staged if staged else forward_plain
    pieces, (rows, qkv_bias, deep) = run(spots, tokens, lengths, shards)
    owned = {name: shards[name].shape[0] if staged else None for name in WEIGHTS}

    one, projected = project(spots, tokens, rows, qkv_bias, pieces[0])
    attended, totals = attend_forward(lengths, projected, 0, pairs)
    third_piece = pieces[2]
    if staged:
        third_piece = gather_z(third_piece, projected)
        near_third = gather_near(third_piece)
        attended = after(attended, third_piece)
    two, middle, three, four, normal, slope = lift(
        spots, attended, tokens, rows, deep[0], deep[1], deep[2], pieces[1]
    )
    if staged:
        third_piece = gather_core(after(near_third, four))
        four = after(four, near_third)
    (down,) = outer(core, four, cotangent, None, "outer_down", jnp.bfloat16)
    if staged:
        middle = after(middle, down)
    out_tokens, up, deep_sums = drop(
        spots, middle, four, normal, slope, cotangent, deep[1], rows[5:6], third_piece
    )
    up_sum = outer(core, three, up, owned["up_weight"], "outer_up")
    if staged:
        up_sum = Sum(spot, *up_sum, "both", "up")
        up = after(up, up_sum.kept)
    total, branch, back, mid_sums = settle(
        spots, up, middle, cotangent, attended, rows[3:4], rows[0:1], pieces[1]
    )
    out_sum = outer(core, two, branch, owned["out_weight"], "outer_out")
    if staged:
        up_sum.add(*out_sum)
        back = after(back, up_sum.chips(back))
    grads = attend_backward(lengths, projected, back, attended, totals, 0)
    qkv_sum = outer_three(core, one, grads, owned["qkv_weight"])
    if staged:
        kept, given = qkv_sum
        flag, up_total = up_sum.plane(kept)
        qkv_sum = Sum(spot, kept, after(given, flag), "both", "qkv")
        total = after(total, qkv_sum.chips())
    grad_tokens, end_sums = finish(spots, *grads, tokens, total, rows[6:7], pieces[0])
    down = lax.psum_scatter(down, AXES, scatter_dimension=0, tiled=True)
    summed = {"down_weight": wide(down)}
    if staged:
        units = 32 * shards["up_bias"].shape[0]
        kept, given = lay_vectors(core, deep_sums, mid_sums, end_sums)
        got = send(given, dc=1)
        flag = qkv_sum.planes(kept, down)
        summed["up_weight"], summed["out_weight"] = jnp.split(up_total, (units,), axis=1)
        summed["qkv_weight"] = qkv_sum.done()
        block = sum_vectors(kept, after(got, flag))
        summed.update({name: block[row, : shards[name].shape[0]] for name, row in SUMMED.items()})
    else:
        deep_rows = 3 * deep.shape[2] // width
        flat = deep_sums[:deep_rows].reshape(3, -1)
        vectors = dict(zip(("hid_gain", "hid_bias", "up_bias"), flat))
        vectors["down_bias"] = deep_sums[deep_rows]
        vectors.update(zip(("ffn_gain", "ffn_bias", "out_bias", "mid_gain", "mid_bias"), mid_sums))
        vectors.update(in_gain=end_sums[0], in_bias=end_sums[1], qv_bias=end_sums[2:4].reshape(-1))
        vectors.update(up_weight=up_sum[0], out_weight=out_sum[0], qkv_weight=qkv_sum[0])
        for name, vector in vectors.items():
            summed[name] = lax.psum_scatter(vector, AXES, scatter_dimension=0, tiled=True)
    return (out_tokens, grad_tokens) + tuple(summed[name] for name in PARAMS)


def solution(mesh):
    staged = (mesh.shape["dp"], mesh.shape["fsdp"]) == (8, 4)
    matrix, vector = P(AXES, None), P(AXES)
    placed = tuple(matrix if name in WEIGHTS else vector for name in PARAMS)
    return jax.shard_map(
        functools.partial(body, staged),
        mesh=mesh,
        in_specs=(matrix,) * 3 + placed,
        out_specs=(matrix,) * 2 + placed,
        check_vma=False,
    )
```

time: 1080 us -> 334 us (0.31)
  waiting for transfers between devices: 663 us -> 54.6 us
  matrix products: 219 us -> 0 us
  Pallas kernels: 0 us -> 191 us
  other arithmetic: 71.9 us -> 6.72 us
  local copies, waits for them, and re-layouts: 65.2 us -> 17.9 us
  starting transfers between devices: 0.57 us -> 45.5 us
  blocking collectives: 43.7 us -> 0 us
    reduce_scatter x4 -> x2, waiting for transfers between devices: 501 us -> 0.01 us  [the longest x1 0.01 us: body(): down = lax.psum_scatter(down, AXES, scatter_dimension=0, tiled=True)]
    dot_general x36 -> x0, matrix products: 219 us -> none  [the longest x6 60.3 us: product(): return jnp.dot(left, right, preferred_element_type=jnp.float32)]
    pallas_call x0 -> x17, Pallas kernels: none -> 191 us  [the longest x1 30.8 us: lift(): pl.pallas_call(functools.partial(lift_kernel, len(weight)), grid=(slots /...]
    all_gather x4 -> x1, waiting for transfers between devices: 87 us -> 0.01 us  [forward_staged(): lax.all_gather(shard, AXES, axis=0, tiled=True)]
    unnamed x10 -> x3, waiting for transfers between devices: 74.2 us -> 0.05 us
    reduce_sum x18 -> x0, other arithmetic: 59.2 us -> none  [the longest x6 23.5 us: layer_norm(): return center * lax.rsqrt(spread + EPSILON) * norm_gain + norm_bias]
    ppermute x0 -> x38, waiting for transfers between devices: none -> 54.5 us  [send(): return lax.ppermute(values, AXES, pairs)]
    ppermute x0 -> x38, starting transfers between devices: none -> 45.3 us  [send(): return lax.ppermute(values, AXES, pairs)]
  transfers between devices with their start and end apart: 9 -> 41, of which waited for: 7 -> 16; matrix products, arithmetic and copies ran while one was open for 17% -> 4% of each run, Pallas kernels for 0% -> 55%
where the time goes in v2:
time: 334 us; the launch traced here: 330 us
  Pallas kernels  191 us (57%)
  waiting for transfers between devices  54.6 us (16%)
  starting transfers between devices  45.5 us (14%)
  local copies, waits for them, and re-layouts  17.9 us (5%)
  between operations  14.6 us (4%)
  other arithmetic  6.72 us (2%)
    ppermute x38, waiting for transfers between devices, send(): return lax.ppermute(values, AXES, pairs)  54.5 us
    ppermute x38, starting transfers between devices, send(): return lax.ppermute(values, AXES, pairs)  45.3 us
    pallas_call x1, Pallas kernels, lift(): pl.pallas_call(functools.partial(lift_kernel, len(weight)), grid=(slots /...  30.8 us
    pallas_call x1, Pallas kernels, drop(): pl.pallas_call(functools.partial(drop_kernel, len(weight)), grid=(slots /...  24 us
    pallas_call x3, Pallas kernels, outer(): pl.pallas_call(functools.partial(outer_kernel, rows), grid=(max(height, c...  23.5 us
    pallas_call x1, Pallas kernels, attend_backward(): pl.pallas_call(functools.partial(attend_back_kernel, tile), grid=(pairs,)...  23.4 us
    pallas_call x1, Pallas kernels, settle(): pl.pallas_call(functools.partial(settle_kernel, len(weight)), grid=(slots...  18.7 us
    pallas_call x1, Pallas kernels, attend_forward(): pl.pallas_call(functools.partial(attend_kernel, tile), grid=(pairs,), out...  16.4 us
  transfers between devices with their start and end apart: 41, of which 16 were waited for; matrix products, arithmetic and copies ran while one was open for 4% of the time, Pallas kernels for 55%

profile of v2, /device:TPU:0, one launch (start us, length us, event | category | flops | bytes accessed | tf_op | source)
XLA Modules:
  0.0 329.9 jit_solution(16295401401112697198)
XLA Ops:
  13.9 3.1 collective-permute-start
  17.0 2.6 collective-permute-start.1
  21.0 2.2 collective-permute-done
  23.2 5.3 %collective-permute-done.1 = bf16[24,2432]{1,0:T(8,128)(2,1)S(1)} collective-permute-done((bf16[24,2432]{1,0:T(8,128)(2,1)S(1)}, bf16[24,2432]{1,0:T(8,128)(2,1)S(1)}, u32[]{:S(2)}, u32[]{:S(2)}) %collective-permute-start.1) | collective-permute-done | bytes 116768 | tf_op jit(solution)/shard_map/ppermute | solution.py:676
  32.2 9.2 %collective-permute-done.4.refs_2_ = bf16[4,24,2432]{2,1,0:T(8,128)(2,1)S(1)} collective-permute-done((bf16[4,24,2432]{2,1,0:T(8,128)(2,1)S(1)}, bf16[4,24,2432]{2,1,0:T(8,128)(2,1)S(1)}, u32[]{:S(2)}, u32[]{:S(2)}) %collective-permute-start.4) | collective-permute-done | bytes 466976 | tf_op jit(solution)/shard_map/ppermute | solution.py:676
  41.4 3.3 collective-permute-done.6.refs_4_
  44.7 12.7 %collective-permute-done.8.refs_6_ = bf16[4,24,2432]{2,1,0:T(8,128)(2,1)S(1)} collective-permute-done((bf16[4,24,2432]{2,1,0:T(8,128)(2,1)S(1)}, bf16[4,24,2432]{2,1,0:T(8,128)(2,1)S(1)}, u32[]{:S(2)}, u32[]{:S(2)}) %collective-permute-start.8) | collective-permute-done | bytes 466976 | tf_op jit(solution)/shard_map/ppermute | solution.py:676
  57.4 4.6 %collective-permute-start.10 = (bf16[96,768]{1,0:T(8,128)(2,1)}, bf16[96,768]{1,0:T(8,128)(2,1)S(1)}, u32[]{:S(2)}, u32[]{:S(2)}) collective-permute-start(bf16[96,768]{1,0:T(8,128)(2,1)} %param.36), channel_id=1, source_target_pairs={{0,8},{1,9},{2,10},{3,11},{4,12},{5,13},{6,14},{7,15},{8,16},{9,17... | collective-permute-start | bytes 442376 | tf_op jit(solution)/shard_map/ppermute | solution.py:676
  62.1 2.4 collective-permute-start.12
  66.0 6.1 %unpack.1 = (f32[8,768]{1,0:T(8,128)}, f32[1,2304]{1,0:T(1,128)}, f32[3,1,3072]{2,1,0:T(1,128)}, bf16[32,24,2304]{2,1,0:T(8,128)(2,1)}) custom-call(s32[32]{0:T(128)} %stack.215.spots_ref, bf16[4,24,2432]{2,1,0:T(8,128)(2,1)} %copy-done.2, bf16[4,24,2432]{2,1,0:T(8,128)(2,1)} %copy-done.18, bf16[4,24,2432]{2,1,0:T(8,128)(2,1)} %copy-done.15, ...), custom_call_target="tpu_custom_call" | custom-call | flops 40000000 | bytes 4000000 | tf_op jit(solution)/shard_map/unpack/pallas_call | solution.py:902
  72.1 10.0 %project.1 = (bf16[1024,768]{1,0:T(8,128)(2,1)}, bf16[1024,2304]{1,0:T(8,128)(2,1)}) custom-call(s32[32]{0:T(128)} %stack.215.spots_ref, bf16[1024,768]{1,0:T(8,128)(2,1)} %x_ref.5, f32[8,768]{1,0:T(8,128)} %get-tuple-element.92.vectors_ref, f32[1,2304]{1,0:T(1,128)} %get-tuple-element.93.bias_ref, bf16[768,2304]{1,0:T(8,128)(2,1)} %bitcast.117), custom_call_target="tpu_custom_call" | custom-call | flops 1449551488 | bytes 6291456 | tf_op jit(solution)/shard_map/project/pallas_call | solution.py:120
  86.7 16.4 %attend_forward.1 = (f32[1024,768]{1,0:T(8,128)}, f32[6,8,1024]{2,1,0:T(8,128)}) custom-call(s32[1,8]{1,0:T(1,128)} %lengths_ref.3, bf16[1024,2304]{1,0:T(8,128)(2,1)} %get-tuple-element.95.q_ref.k_ref.v_ref, bf16[1024,2304]{1,0:T(8,128)(2,1)} %get-tuple-element.95.q_ref.k_ref.v_ref, bf16[1024,2304]{1,0:T(8,128)(2,1)} %get-tuple-element.95.q_ref.k_ref.v_ref), custom_call_target="tpu_custom_call" | custom-call | flops 8000000000 | bytes 3200000 | tf_op jit(solution)/shard_map/attend_forward/pallas_call | solution.py:566
  103.8 30.8 %lift.1 = (bf16[1024,768]{1,0:T(8,128)(2,1)}, f32[1024,768]{1,0:T(8,128)}, bf16[1024,768]{1,0:T(8,128)(2,1)}, bf16[1024,3072]{1,0:T(8,128)(2,1)}, bf16[1024,3072...) custom-call(s32[32]{0:T(128)} %stack.215.spots_ref, f32[1024,768]{1,0:T(8,128)} %get-tuple-element.102.attended_ref.out_ref, ...), custom_call_target="tpu_custom_call" | custom-call | flops 2415919104 | bytes 12582912 | tf_op jit(solution)/shard_map/lift/pallas_call | solution.py:204
  134.7 9.7 %outer_down.1 = bf16[3072,768]{1,0:T(8,128)(2,1)} custom-call(s32[1]{0:T(128)} %bitcast.56.core_ref, bf16[1024,3072]{1,0:T(8,128)(2,1)} %get-tuple-element.106.left_ref.four_ref, bf16[1024,768]{1,0:T(8,128)(2,1)} %grad_ref.3), custom_call_target="tpu_custom_call" | custom-call | flops 1932735232 | bytes 6920601 | tf_op jit(solution)/shard_map/outer_down/pallas_call | solution.py:459
  149.9 24.0 %drop.1 = (bf16[1024,768]{1,0:T(8,128)(2,1)}, bf16[1024,3072]{1,0:T(8,128)(2,1)}, f32[13,768]{1,0:T(8,128)}) custom-call(s32[32]{0:T(128)} %stack.215.spots_ref, f32[1024,768]{1,0:T(8,128)} %get-tuple-element.107.middle_ref, bf16[1024,3072]{1,0:T(8,128)(2,1)} %get-tuple-element.106.left_ref.four_ref, bf16[1024,3072]{1,0:T(8,128)(2,1)} %get-tuple-element.108.normal_ref, ...), custom_call_target="tpu_custom_call" | custom-call | flops 3865470464 | bytes 12582912 | tf_op jit(solution)/shard_map/drop/pallas_call | solution.py:285
  173.9 9.4 %outer_up.1 = (bf16[16,24,3072]{2,1,0:T(8,128)(2,1)}, bf16[16,24,3072]{2,1,0:T(8,128)(2,1)}) custom-call(s32[1]{0:T(128)} %bitcast.56.core_ref, bf16[1024,768]{1,0:T(8,128)(2,1)} %get-tuple-element.116.left_ref, bf16[1024,3072]{1,0:T(8,128)(2,1)} %get-tuple-element.118.right_ref.up_ref), custom_call_target="tpu_custom_call" | custom-call | flops 1932735232 | bytes 6920601 | tf_op jit(solution)/shard_map/outer_up/pallas_call | solution.py:459
  183.5 18.7 %settle.1 = (f32[1024,768]{1,0:T(8,128)}, bf16[1024,768]{1,0:T(8,128)(2,1)}, bf16[1024,768]{1,0:T(8,128)(2,1)}, f32[8,768]{1,0:T(8,128)}) custom-call(s32[32]{0:T(128)} %stack.215.spots_ref, bf16[1024,3072]{1,0:T(8,128)(2,1)} %get-tuple-element.118.right_ref.up_ref, f32[1024,768]{1,0:T(8,128)} %get-tuple-element.107.middle_ref, bf16[1024,768]{1,0:T(8,128)(2,1)} %grad_ref.3, ...), custom_call_target="tpu_custom_call" | custom-call | flops 2415919104 | bytes 9437184 | tf_op jit(solution)/shard_map/settle/pallas_call | solution.py:350
  202.2 4.4 %outer_out.1 = (bf16[16,24,768]{2,1,0:T(8,128)(2,1)}, bf16[16,24,768]{2,1,0:T(8,128)(2,1)}) custom-call(s32[1]{0:T(128)} %bitcast.56.core_ref, bf16[1024,768]{1,0:T(8,128)(2,1)} %get-tuple-element.122.left_ref, bf16[1024,768]{1,0:T(8,128)(2,1)} %get-tuple-element.123.right_ref), custom_call_target="tpu_custom_call" | custom-call | flops 483183808 | bytes 2202009 | tf_op jit(solution)/shard_map/outer_out/pallas_call | solution.py:459
  210.3 5.0 %chips_up.1 = (bf16[4,24,3840]{2,1,0:T(8,128)(2,1)}, bf16[4,24,3840]{2,1,0:T(8,128)(2,1)}, bf16[4,24,3840]{2,1,0:T(8,128)(2,1)}, bf16[4,24,3840]{2,1,0:T(8,128)(2,1)}) custom-call(s32[4]{0:T(128)} %pad_add_fusion.place_ref, bf16[16,24,3072]{2,1,0:T(8,128)(2,1)} %get-tuple-element.120.refs_0_, bf16[16,24,3072]{2,1,0:T(8,128)(2,1)} %copy-done.1, ...), custom_call_target="tpu_custom_call" | custom-call | bytes 3538944 | tf_op jit(solution)/shard_map/chips_up/pallas_call | solution.py:772
  218.8 23.4 %attend_backward.1 = (bf16[1024,768]{1,0:T(8,128)(2,1)}, bf16[1024,768]{1,0:T(8,128)(2,1)}, bf16[1024,768]{1,0:T(8,128)(2,1)}) custom-call(s32[1,8]{1,0:T(1,128)} %lengths_ref.3, bf16[1024,2304]{1,0:T(8,128)(2,1)} %get-tuple-element.95.q_ref.k_ref.v_ref, bf16[1024,2304]{1,0:T(8,128)(2,1)} %get-tuple-element.95.q_ref.k_ref.v_ref, ...), custom_call_target="tpu_custom_call" | custom-call | flops 11200000000 | bytes 4800000 | tf_op jit(solution)/shard_map/attend_backward/pallas_call | solution.py:636
  242.2 8.5 %outer_three.1 = (bf16[16,24,2304]{2,1,0:T(8,128)(2,1)}, bf16[16,24,2304]{2,1,0:T(8,128)(2,1)}) custom-call(s32[1]{0:T(128)} %bitcast.56.core_ref, bf16[1024,768]{1,0:T(8,128)(2,1)} %get-tuple-element.133.left_ref, bf16[1024,768]{1,0:T(8,128)(2,1)} %get-tuple-element.129.q_ref, bf16[1024,768]{1,0:T(8,128)(2,1)} %get-tuple-element.130.k_ref, ...), custom_call_target="tpu_custom_call" | custom-call | flops 1449551488 | bytes 5347737 | tf_op jit(solution)/shard_map/outer_three/pallas_call | solution.py:493
  250.7 4.7 %collective-permute-done.22.refs_1_ = bf16[4,24,3840]{2,1,0:T(8,128)(2,1)S(1)} collective-permute-done((bf16[4,24,3840]{2,1,0:T(8,128)(2,1)}, bf16[4,24,3840]{2,1,0:T(8,128)(2,1)S(1)}, u32[]{:S(2)}, u32[]{:S(2)}) %collective-permute-start.22) | collective-permute-done | bytes 737312 | tf_op jit(solution)/shard_map/ppermute | solution.py:676
  257.4 3.0 plane_up.1
  260.5 3.7 %collective-permute-done.25.refs_1_ = bf16[16,24,2304]{2,1,0:T(8,128)(2,1)S(1)} collective-permute-done((bf16[16,24,2304]{2,1,0:T(8,128)(2,1)S(1)}, bf16[16,24,2304]{2,1,0:T(8,128)(2,1)S(1)}, u32[]{:S(2)}, u32[]{:S(2)}) %collective-permute-start.25) | collective-permute-done | bytes 1769504 | tf_op jit(solution)/shard_map/ppermute | solution.py:676
  265.3 3.6 %chips_qkv.1 = (bf16[4,24,2304]{2,1,0:T(8,128)(2,1)}, bf16[4,24,2304]{2,1,0:T(8,128)(2,1)}, bf16[4,24,2304]{2,1,0:T(8,128)(2,1)}, bf16[4,24,2304]{2,1,0:T(8,128)(2,1)}) custom-call(s32[4]{0:T(128)} %pad_add_fusion.place_ref, bf16[16,24,2304]{2,1,0:T(8,128)(2,1)} %get-tuple-element.134.refs_0_, bf16[16,24,2304]{2,1,0:T(8,128)(2,1)} %copy-done.3), custom_call_target="tpu_custom_call" | custom-call | bytes 2123366 | tf_op jit(solution)/shard_map/chips_qkv/pallas_call | solution.py:772
  272.4 11.7 %finish.1 = (f32[1024,768]{1,0:T(8,128)}, f32[8,768]{1,0:T(8,128)}) custom-call(s32[32]{0:T(128)} %stack.215.spots_ref, bf16[1024,768]{1,0:T(8,128)(2,1)} %get-tuple-element.129.q_ref, bf16[1024,768]{1,0:T(8,128)(2,1)} %get-tuple-element.130.k_ref, bf16[1024,768]{1,0:T(8,128)(2,1)} %get-tuple-element.131.v_ref, bf16[1024,768]{1,0:T(8,128)(2,1)} %x_ref.5, ...), custom_call_target="tpu_custom_call" | custom-call | flops 1449551488 | bytes 7549747 | tf_op jit(solution)/shard_map/finish/pallas_call | solution.py:405
  284.1 3.7 %owners.1 = (f32[16,24,128]{2,1,0:T(8,128)}, f32[16,24,128]{2,1,0:T(8,128)}) custom-call(s32[1]{0:T(128)} %bitcast.56.core_ref, f32[13,768]{1,0:T(8,128)} %get-tuple-element.144.deep_ref, f32[8,768]{1,0:T(8,128)} %get-tuple-element.145.mid_ref, f32[8,768]{1,0:T(8,128)} %get-tuple-element.146.end_ref), custom_call_target="tpu_custom_call" | custom-call | bytes 400000 | tf_op jit(solution)/shard_map/owners/pallas_call | solution.py:979
  287.9 4.1 %collective-permute-done.29.refs_3_ = bf16[4,24,2304]{2,1,0:T(8,128)(2,1)S(1)} collective-permute-done((bf16[4,24,2304]{2,1,0:T(8,128)(2,1)}, bf16[4,24,2304]{2,1,0:T(8,128)(2,1)S(1)}, u32[]{:S(2)}, u32[]{:S(2)}) %collective-permute-start.29) | collective-permute-done | bytes 442400 | tf_op jit(solution)/shard_map/ppermute | solution.py:676
  292.8 2.3 planes_qkv.1
  297.8 3.0 collective-permute-done.30
  305.6 5.9 %collective-permute-start.35 = (bf16[24,2304]{1,0:T(8,128)(2,1)}, bf16[24,2304]{1,0:T(8,128)(2,1)S(1)}, u32[]{:S(2)}, u32[]{:S(2)}) collective-permute-start(bf16[24,2304]{1,0:T(8,128)(2,1)} %get-tuple-element.155), channel_id=1, source_target_pairs={{0,8},{1,9},{2,10},{3,11},{4,12},{5,13},{6,14},{7,15},{8,16},{9,17... | collective-permute-start | bytes 331784 | tf_op jit(solution)/shard_map/ppermute | solution.py:676
  315.2 2.0 collective-permute-start.33
  (159 shorter events, 55.8 us)
Async XLA Ops:
  7.2 96.6 %all-gather.2.cloned.1.call-start = ((), (), s32[]{:S(2)}) async-start(), calls=%async_computation.2 | async-start | bytes 6082560 | tf_op jit(solution)/shard_map/all_gather | solution.py:1029
  8.9 279.0 %reduce-scatter.3.cloned.1.call-start = ((), (), s32[]{:S(2)}) async-start(), calls=%async_computation.3 | async-start | bytes 4866048 | tf_op jit(solution)/shard_map/reduce_scatter | solution.py:1104
  13.9 9.2 %collective-permute-start = (bf16[24,2432]{1,0:T(8,128)(2,1)S(1)}, bf16[24,2432]{1,0:T(8,128)(2,1)S(1)}, u32[]{:S(2)}, u32[]{:S(2)}) collective-permute-start(bf16[24,2432]{1,0:T(8,128)(2,1)S(1)} %fusion.1), channel_id=1, source_target_pairs={{0,8},{1,9},{2,10},{3,11},{4,12},{5,13},{6,14},{7,15},{8,16},{9,17... | collective-permute-start | bytes 350216 | tf_op jit(solution)/shard_map/ppermute | solution.py:676
  17.0 11.5 %collective-permute-start.1 = (bf16[24,2432]{1,0:T(8,128)(2,1)S(1)}, bf16[24,2432]{1,0:T(8,128)(2,1)S(1)}, u32[]{:S(2)}, u32[]{:S(2)}) collective-permute-start(bf16[24,2432]{1,0:T(8,128)(2,1)S(1)} %fusion.1), channel_id=1, source_target_pairs={{0,16},{1,17},{2,18},{3,19},{4,20},{5,21},{6,22},{7,23},{8,24},{9,... | collective-permute-start | bytes 350216 | tf_op jit(solution)/shard_map/ppermute | solution.py:676
  19.6 8.9 %collective-permute-start.2 = (bf16[24,2432]{1,0:T(8,128)(2,1)S(1)}, bf16[24,2432]{1,0:T(8,128)(2,1)S(1)}, u32[]{:S(2)}, u32[]{:S(2)}) collective-permute-start(bf16[24,2432]{1,0:T(8,128)(2,1)S(1)} %fusion.1), channel_id=1, source_target_pairs={{0,24},{1,25},{2,26},{3,27},{4,28},{5,29},{6,30},{7,31},{8,0},{9,1... | collective-permute-start | bytes 350216 | tf_op jit(solution)/shard_map/ppermute | solution.py:676
  28.6 12.8 %collective-permute-start.4 = (bf16[4,24,2432]{2,1,0:T(8,128)(2,1)S(1)}, bf16[4,24,2432]{2,1,0:T(8,128)(2,1)S(1)}, u32[]{:S(2)}, u32[]{:S(2)}) collective-permute-start(bf16[4,24,2432]{2,1,0:T(8,128)(2,1)S(1)} %pad_maximum_fusion.1.refs_0_), channel_id=1, source_target_pairs={{0,2},{1,3},{2,0},{3,1},{4,6},{5,7},{6,4},{7,5},{8,10},{9,11},{10,... | collective-permute-start | bytes 1400840 | tf_op jit(solution)/shard_map/ppermute | solution.py:676
  30.3 14.4 %collective-permute-start.6 = (bf16[4,24,2432]{2,1,0:T(8,128)(2,1)S(1)}, bf16[4,24,2432]{2,1,0:T(8,128)(2,1)S(1)}, u32[]{:S(2)}, u32[]{:S(2)}) collective-permute-start(bf16[4,24,2432]{2,1,0:T(8,128)(2,1)S(1)} %pad_maximum_fusion.1.refs_0_), channel_id=1, source_target_pairs={{0,4},{1,5},{2,6},{3,7},{4,0},{5,1},{6,2},{7,3},{8,12},{9,13},{10,... | collective-permute-start | bytes 1400840 | tf_op jit(solution)/shard_map/ppermute | solution.py:676
  31.8 25.6 %collective-permute-start.8 = (bf16[4,24,2432]{2,1,0:T(8,128)(2,1)S(1)}, bf16[4,24,2432]{2,1,0:T(8,128)(2,1)S(1)}, u32[]{:S(2)}, u32[]{:S(2)}) collective-permute-start(bf16[4,24,2432]{2,1,0:T(8,128)(2,1)S(1)} %pad_maximum_fusion.1.refs_0_), channel_id=1, source_target_pairs={{0,6},{1,7},{2,4},{3,5},{4,2},{5,3},{6,0},{7,1},{8,14},{9,15},{10,... | collective-permute-start | bytes 1400840 | tf_op jit(solution)/shard_map/ppermute | solution.py:676
  32.2 29.9 %collective-permute-start.3 = (bf16[4,24,2432]{2,1,0:T(8,128)(2,1)S(1)}, bf16[4,24,2432]{2,1,0:T(8,128)(2,1)S(1)}, u32[]{:S(2)}, u32[]{:S(2)}) collective-permute-start(bf16[4,24,2432]{2,1,0:T(8,128)(2,1)S(1)} %pad_maximum_fusion.1.refs_0_), channel_id=1, source_target_pairs={{0,1},{1,0},{2,3},{3,2},{4,5},{5,4},{6,7},{7,6},{8,9},{9,8},{10,11... | collective-permute-start | bytes 1400840 | tf_op jit(solution)/shard_map/ppermute | solution.py:676
  41.4 20.6 %collective-permute-start.5 = (bf16[4,24,2432]{2,1,0:T(8,128)(2,1)S(1)}, bf16[4,24,2432]{2,1,0:T(8,128)(2,1)S(1)}, u32[]{:S(2)}, u32[]{:S(2)}) collective-permute-start(bf16[4,24,2432]{2,1,0:T(8,128)(2,1)S(1)} %collective-permute-done.4.refs_2_), channel_id=1, source_target_pairs={{0,1},{1,0},{2,3},{3,2},{4,5},{5,4},{6,7},{7,6},{8,9},{9,8},{10,11... | collective-permute-start | bytes 1400840 | tf_op jit(solution)/shard_map/ppermute | solution.py:676
  44.7 20.5 %collective-permute-start.7 = (bf16[4,24,2432]{2,1,0:T(8,128)(2,1)S(1)}, bf16[4,24,2432]{2,1,0:T(8,128)(2,1)S(1)}, u32[]{:S(2)}, u32[]{:S(2)}) collective-permute-start(bf16[4,24,2432]{2,1,0:T(8,128)(2,1)S(1)} %collective-permute-done.6.refs_4_), channel_id=1, source_target_pairs={{0,1},{1,0},{2,3},{3,2},{4,5},{5,4},{6,7},{7,6},{8,9},{9,8},{10,11... | collective-permute-start | bytes 1400840 | tf_op jit(solution)/shard_map/ppermute | solution.py:676
  57.4 7.8 %collective-permute-start.9 = (bf16[4,24,2432]{2,1,0:T(8,128)(2,1)S(1)}, bf16[4,24,2432]{2,1,0:T(8,128)(2,1)}, u32[]{:S(2)}, u32[]{:S(2)}) collective-permute-start(bf16[4,24,2432]{2,1,0:T(8,128)(2,1)S(1)} %collective-permute-done.8.refs_6_), channel_id=1, source_target_pairs={{0,1},{1,0},{2,3},{3,2},{4,5},{5,4},{6,7},{7,6},{8,9},{9,8},{10,11... | collective-permute-start | bytes 1400840 | tf_op jit(solution)/shard_map/ppermute | solution.py:676
  57.4 24.7 %collective-permute-start.10 = (bf16[96,768]{1,0:T(8,128)(2,1)}, bf16[96,768]{1,0:T(8,128)(2,1)S(1)}, u32[]{:S(2)}, u32[]{:S(2)}) collective-permute-start(bf16[96,768]{1,0:T(8,128)(2,1)} %param.36), channel_id=1, source_target_pairs={{0,8},{1,9},{2,10},{3,11},{4,12},{5,13},{6,14},{7,15},{8,16},{9,17... | collective-permute-start | bytes 442376 | tf_op jit(solution)/shard_map/ppermute | solution.py:676
  62.0 20.0 %collective-permute-start.11 = (bf16[96,768]{1,0:T(8,128)(2,1)}, bf16[96,768]{1,0:T(8,128)(2,1)}, u32[]{:S(2)}, u32[]{:S(2)}) collective-permute-start(bf16[96,768]{1,0:T(8,128)(2,1)} %param.36), channel_id=1, source_target_pairs={{0,16},{1,17},{2,18},{3,19},{4,20},{5,21},{6,22},{7,23},{8,24},{9,... | collective-permute-start | bytes 442376 | tf_op jit(solution)/shard_map/ppermute | solution.py:676
  62.1 20.0 %collective-permute-start.12 = (bf16[96,768]{1,0:T(8,128)(2,1)}, bf16[96,768]{1,0:T(8,128)(2,1)}, u32[]{:S(2)}, u32[]{:S(2)}) collective-permute-start(bf16[96,768]{1,0:T(8,128)(2,1)} %param.36), channel_id=1, source_target_pairs={{0,24},{1,25},{2,26},{3,27},{4,28},{5,29},{6,30},{7,31},{8,0},{9,1... | collective-permute-start | bytes 442376 | tf_op jit(solution)/shard_map/ppermute | solution.py:676
  83.2 51.4 %collective-permute-start.13 = (bf16[4,96,768]{2,1,0:T(8,128)(2,1)S(1)}, bf16[4,96,768]{2,1,0:T(8,128)(2,1)S(1)}, u32[]{:S(2)}, u32[]{:S(2)}) collective-permute-start(bf16[4,96,768]{2,1,0:T(8,128)(2,1)S(1)} %pad_maximum_fusion.refs_0_), channel_id=1, source_target_pairs={{0,2},{1,3},{2,0},{3,1},{4,6},{5,7},{6,4},{7,5},{8,10},{9,11},{10,... | collective-permute-start | bytes 1769480 | tf_op jit(solution)/shard_map/ppermute | solution.py:676
  84.8 49.8 %collective-permute-start.14 = (bf16[4,96,768]{2,1,0:T(8,128)(2,1)S(1)}, bf16[4,96,768]{2,1,0:T(8,128)(2,1)S(1)}, u32[]{:S(2)}, u32[]{:S(2)}) collective-permute-start(bf16[4,96,768]{2,1,0:T(8,128)(2,1)S(1)} %pad_maximum_fusion.refs_0_), channel_id=1, source_target_pairs={{0,4},{1,5},{2,6},{3,7},{4,0},{5,1},{6,2},{7,3},{8,12},{9,13},{10,... | collective-permute-start | bytes 1769480 | tf_op jit(solution)/shard_map/ppermute | solution.py:676
  86.3 48.3 %collective-permute-start.15 = (bf16[4,96,768]{2,1,0:T(8,128)(2,1)S(1)}, bf16[4,96,768]{2,1,0:T(8,128)(2,1)S(1)}, u32[]{:S(2)}, u32[]{:S(2)}) collective-permute-start(bf16[4,96,768]{2,1,0:T(8,128)(2,1)S(1)} %pad_maximum_fusion.refs_0_), channel_id=1, source_target_pairs={{0,6},{1,7},{2,4},{3,5},{4,2},{5,3},{6,0},{7,1},{8,14},{9,15},{10,... | collective-permute-start | bytes 1769480 | tf_op jit(solution)/shard_map/ppermute | solution.py:676
  144.5 158.1 %reduce-scatter.5.cloned.1.call-start = ((), (), s32[]{:S(2)}) async-start(), calls=%async_computation.4 | async-start | bytes 921600 | tf_op jit(solution)/shard_map/reduce_scatter | solution.py:834
  183.3 25.4 %collective-permute-start.20 = (bf16[16,24,3072]{2,1,0:T(8,128)(2,1)}, bf16[16,24,3072]{2,1,0:T(8,128)(2,1)S(1)}, u32[]{:S(2)}, u32[]{:S(2)}) collective-permute-start(bf16[16,24,3072]{2,1,0:T(8,128)(2,1)} %get-tuple-element.121), channel_id=1, source_target_pairs={{0,1},{1,0},{2,3},{3,2},{4,5},{5,4},{6,7},{7,6},{8,9},{9,8},{10,11... | collective-permute-start | bytes 7077896 | tf_op jit(solution)/shard_map/ppermute | solution.py:676
  215.3 40.0 %collective-permute-start.22 = (bf16[4,24,3840]{2,1,0:T(8,128)(2,1)}, bf16[4,24,3840]{2,1,0:T(8,128)(2,1)S(1)}, u32[]{:S(2)}, u32[]{:S(2)}) collective-permute-start(bf16[4,24,3840]{2,1,0:T(8,128)(2,1)} %get-tuple-element.137), channel_id=1, source_target_pairs={{0,2},{1,3},{2,0},{3,1},{4,6},{5,7},{6,4},{7,5},{8,10},{9,11},{10,... | collective-permute-start | bytes 2211848 | tf_op jit(solution)/shard_map/ppermute | solution.py:676
  217.1 38.3 %collective-permute-start.23 = (bf16[4,24,3840]{2,1,0:T(8,128)(2,1)}, bf16[4,24,3840]{2,1,0:T(8,128)(2,1)S(1)}, u32[]{:S(2)}, u32[]{:S(2)}) collective-permute-start(bf16[4,24,3840]{2,1,0:T(8,128)(2,1)} %get-tuple-element.138), channel_id=1, source_target_pairs={{0,4},{1,5},{2,6},{3,7},{4,0},{5,1},{6,2},{7,3},{8,12},{9,13},{10,... | collective-permute-start | bytes 2211848 | tf_op jit(solution)/shard_map/ppermute | solution.py:676
  218.4 37.0 %collective-permute-start.24 = (bf16[4,24,3840]{2,1,0:T(8,128)(2,1)}, bf16[4,24,3840]{2,1,0:T(8,128)(2,1)S(1)}, u32[]{:S(2)}, u32[]{:S(2)}) collective-permute-start(bf16[4,24,3840]{2,1,0:T(8,128)(2,1)} %get-tuple-element.139), channel_id=1, source_target_pairs={{0,6},{1,7},{2,4},{3,5},{4,2},{5,3},{6,0},{7,1},{8,14},{9,15},{10,... | collective-permute-start | bytes 2211848 | tf_op jit(solution)/shard_map/ppermute | solution.py:676
  268.9 18.9 %collective-permute-start.27 = (bf16[4,24,2304]{2,1,0:T(8,128)(2,1)}, bf16[4,24,2304]{2,1,0:T(8,128)(2,1)S(1)}, u32[]{:S(2)}, u32[]{:S(2)}) collective-permute-start(bf16[4,24,2304]{2,1,0:T(8,128)(2,1)} %get-tuple-element.150), channel_id=1, source_target_pairs={{0,2},{1,3},{2,0},{3,1},{4,6},{5,7},{6,4},{7,5},{8,10},{9,11},{10,... | collective-permute-start | bytes 1327112 | tf_op jit(solution)/shard_map/ppermute | solution.py:676
  270.6 17.3 %collective-permute-start.28 = (bf16[4,24,2304]{2,1,0:T(8,128)(2,1)}, bf16[4,24,2304]{2,1,0:T(8,128)(2,1)S(1)}, u32[]{:S(2)}, u32[]{:S(2)}) collective-permute-start(bf16[4,24,2304]{2,1,0:T(8,128)(2,1)} %get-tuple-element.151), channel_id=1, source_target_pairs={{0,4},{1,5},{2,6},{3,7},{4,0},{5,1},{6,2},{7,3},{8,12},{9,13},{10,... | collective-permute-start | bytes 1327112 | tf_op jit(solution)/shard_map/ppermute | solution.py:676
  272.0 20.0 %collective-permute-start.29 = (bf16[4,24,2304]{2,1,0:T(8,128)(2,1)}, bf16[4,24,2304]{2,1,0:T(8,128)(2,1)S(1)}, u32[]{:S(2)}, u32[]{:S(2)}) collective-permute-start(bf16[4,24,2304]{2,1,0:T(8,128)(2,1)} %get-tuple-element.152), channel_id=1, source_target_pairs={{0,6},{1,7},{2,4},{3,5},{4,2},{5,3},{6,0},{7,1},{8,14},{9,15},{10,... | collective-permute-start | bytes 1327112 | tf_op jit(solution)/shard_map/ppermute | solution.py:676
  287.8 7.2 %collective-permute-start.26 = (f32[16,24,128]{2,1,0:T(8,128)}, f32[16,24,128]{2,1,0:T(8,128)S(1)}, u32[]{:S(2)}, u32[]{:S(2)}) collective-permute-start(f32[16,24,128]{2,1,0:T(8,128)} %get-tuple-element.148), channel_id=1, source_target_pairs={{0,1},{1,0},{2,3},{3,2},{4,5},{5,4},{6,7},{7,6},{8,9},{9,8},{10,11... | collective-permute-start | bytes 589832 | tf_op jit(solution)/shard_map/ppermute | solution.py:676
  300.8 13.8 %collective-permute-start.31 = (f32[4,24,128]{2,1,0:T(8,128)S(1)}, f32[4,24,128]{2,1,0:T(8,128)S(1)}, u32[]{:S(2)}, u32[]{:S(2)}) collective-permute-start(f32[4,24,128]{2,1,0:T(8,128)S(1)} %dynamic-slice_bitcast_fusion.1), channel_id=1, source_target_pairs={{0,2},{1,3},{2,0},{3,1},{4,6},{5,7},{6,4},{7,5},{8,10},{9,11},{10,... | collective-permute-start | bytes 147464 | tf_op jit(solution)/shard_map/ppermute | solution.py:676
  305.6 11.7 %collective-permute-start.35 = (bf16[24,2304]{1,0:T(8,128)(2,1)}, bf16[24,2304]{1,0:T(8,128)(2,1)S(1)}, u32[]{:S(2)}, u32[]{:S(2)}) collective-permute-start(bf16[24,2304]{1,0:T(8,128)(2,1)} %get-tuple-element.155), channel_id=1, source_target_pairs={{0,8},{1,9},{2,10},{3,11},{4,12},{5,13},{6,14},{7,15},{8,16},{9,17... | collective-permute-start | bytes 331784 | tf_op jit(solution)/shard_map/ppermute | solution.py:676
  311.5 8.3 %collective-permute-start.36 = (bf16[24,2304]{1,0:T(8,128)(2,1)}, bf16[24,2304]{1,0:T(8,128)(2,1)S(1)}, u32[]{:S(2)}, u32[]{:S(2)}) collective-permute-start(bf16[24,2304]{1,0:T(8,128)(2,1)} %get-tuple-element.156), channel_id=1, source_target_pairs={{0,16},{1,17},{2,18},{3,19},{4,20},{5,21},{6,22},{7,23},{8,24},{9,... | collective-permute-start | bytes 331784 | tf_op jit(solution)/shard_map/ppermute | solution.py:676
  312.3 7.4 %collective-permute-start.37 = (bf16[24,2304]{1,0:T(8,128)(2,1)}, bf16[24,2304]{1,0:T(8,128)(2,1)S(1)}, u32[]{:S(2)}, u32[]{:S(2)}) collective-permute-start(bf16[24,2304]{1,0:T(8,128)(2,1)} %get-tuple-element.157), channel_id=1, source_target_pairs={{0,24},{1,25},{2,26},{3,27},{4,28},{5,29},{6,30},{7,31},{8,0},{9,1... | collective-permute-start | bytes 331784 | tf_op jit(solution)/shard_map/ppermute | solution.py:676
  315.2 6.2 %collective-permute-start.33 = (f32[24,128]{1,0:T(8,128)S(1)}, f32[24,128]{1,0:T(8,128)S(1)}, u32[]{:S(2)}, u32[]{:S(2)}) collective-permute-start(f32[24,128]{1,0:T(8,128)S(1)} %get-tuple-element.158), channel_id=1, source_target_pairs={{0,16},{1,17},{2,18},{3,19},{4,20},{5,21},{6,22},{7,23},{8,24},{9,... | collective-permute-start | bytes 36872 | tf_op jit(solution)/shard_map/ppermute | solution.py:676
  (39 other events, 334.0 us)
Sparse Core Ops, SparseCore 0:
  11.5 80.0 all-gather.1
  144.6 122.6 reduce-scatter.2
  269.6 22.8 reduce-scatter.4
